TPU v7x, 128 devices: a whole 4x4x4 slice. The times are simulated.
128 devices in a mesh: child: 4 (over y), row: 4 (over x), col: 8 (over z, core).
Axes of the slice: x: 4, y: 4, z: 4, core: 2. Of those that a mesh axis runs over, the one named last changes fastest.
Arguments:
- parent_solution: float32 [16384, 256], P(('child', 'row', 'col')), may hold values from -6 to 6
- border_owner: int32 [4, 8192, 1], replicated, may hold values from 0 to 127; in each aligned block of 256 rows (0 to 255, 256 to 511, ..., all dimensions but the last counted through in order) at most 4 rows name the same one
- border_slot: int32 [4, 8192], replicated, may hold values from 0 to 127
- border_tile: float32 [4, 8192, 8192], P('child', 'row', 'col'), may hold values from -0.0625 to 0.0625
- pivot_inverse: float32 [4, 8192, 8192], P('child', 'row', 'col'), may hold values from -0.0625 to 0.0625
- pivot_rhs: float32 [4, 8192, 256], P('child', 'col'), may hold values from -6 to 6
Outputs:
- pivot_solution: float32 [4, 8192, 256], P('child', ('row', 'col'))
Inputs may be any that keep to these rules, and one draw needn't show every extreme that they name: `border_owner`: within each aligned block of 256 border rows of one front, no device is named more than 4 times, and some device is named exactly 4 times in some blocks.
All inputs are finite; a program needn't handle non-finite values.
Results may differ from a plain program's by a relative error of at most 0.0003.
Values sent between devices are 32-bit elements; how exact they have to be, the bound alone decides.
No kernel may reach another device: no remote copies, remote signals or barrier semaphores. Data moves between devices by JAX's collectives and lax.ppermute only.
A program may use at most 128 MiB of HBM per device.

v0:
```python
import functools

import jax
import jax.numpy as jnp
from jax import lax
from jax.experimental import pallas as pl
from jax.experimental.pallas import tpu as pltpu
from jax.sharding import PartitionSpec as P

F32 = jnp.float32
BF16 = jnp.bfloat16
I32 = jnp.int32
SLOTS = 4


def dot(a, b):
    return jnp.dot(a, b, preferred_element_type=F32)


def split2(x):
    hi = x.astype(BF16)
    return hi, (x - hi.astype(F32)).astype(BF16)


def split3(x):
    hi = x.astype(BF16)
    rest = x - hi.astype(F32)
    mid = rest.astype(BF16)
    return hi, mid, (rest - mid.astype(F32)).astype(BF16)


def ones_upto(n):
    rows = lax.broadcasted_iota(I32, (n, n), 0)
    cols = lax.broadcasted_iota(I32, (n, n), 1)
    return jnp.where(rows <= cols, 1.0, 0.0).astype(BF16)


def indicator(flag):
    return jnp.where(flag, 1.0, 0.0).astype(BF16)


def pick_kernel(idx_ref, owner_ref, slot_ref, parent_ref, out_ref):
    me = idx_ref[0]
    blocks = owner_ref.shape[0] // 2
    lanes = owner_ref.shape[1]
    upto = ones_upto(lanes)
    parts = [split3(parent_ref[:, h * lanes:(h + 1) * lanes]) for h in range(2)]
    mask = [owner_ref[pl.ds(h, blocks, stride=2), :] == me for h in range(2)]
    slot = []
    children = 4
    per_child = blocks // children
    for h in range(2):
        slot.append(jnp.concatenate(
            [slot_ref[pl.ds(children * h + c, per_child, stride=2 * children), :]
             for c in range(children)], axis=0))
    count0 = dot(indicator(mask[0]), upto)
    count1 = dot(indicator(mask[1]), upto) + count0[:, lanes - 1:lanes]
    count = [count0, count1]
    local = lax.broadcasted_iota(I32, (blocks, lanes), 1)
    for p in range(SLOTS):
        asked = jnp.zeros((blocks, 1), I32)
        for h in range(2):
            chosen = mask[h] & (count[h] == float(p + 1))
            asked = asked + jnp.sum(jnp.where(chosen, slot[h] + 1, 0), axis=1, keepdims=True)
        select = indicator(local + 1 == asked)
        for h in range(2):
            hi, mid, lo = parts[h]
            out_ref[pl.ds(2 * p + h, blocks, stride=2 * SLOTS), :] = (
                dot(select, lo) + dot(select, mid)) + dot(select, hi)


def place_kernel(idx_ref, owner_ref, got_ref, out_ref):
    me = idx_ref[0]
    lanes = owner_ref.shape[1]
    devices = got_ref.shape[0] // (2 * SLOTS)
    upto = ones_upto(lanes)
    source = lax.broadcasted_iota(I32, (devices, lanes), 0)
    flag = [source == owner_ref[pl.ds(2 * me + h, 1), :] for h in range(2)]
    count0 = dot(indicator(flag[0]), upto)
    count1 = dot(indicator(flag[1]), upto) + count0[:, lanes - 1:lanes]
    count = [count0, count1]
    for half in range(2):
        acc = [jnp.zeros((lanes, lanes), F32) for _ in range(2)]
        for p in range(SLOTS):
            rows = got_ref[pl.ds(2 * p + half, devices, stride=2 * SLOTS), :]
            parts = split3(rows.T)
            for h in range(2):
                choose = indicator(flag[h] & (count[h] == float(p + 1)))
                for part in parts:
                    acc[h] = acc[h] + dot(part, choose)
        for h in range(2):
            out_ref[half * lanes:(half + 1) * lanes, h * lanes:(h + 1) * lanes] = acc[h]


def couple_kernel(idx_ref, values_ref, tile_ref, *outs):
    s = pl.program_id(0)
    blocks, loads, rows = values_ref.shape
    acc = None
    for b in range(blocks):
        vh, vl = split2(values_ref[b])
        th, tl = split2(tile_ref[b * rows:(b + 1) * rows, :])
        part = dot(vh, th) + (dot(vh, tl) + dot(vl, th))
        acc = part if acc is None else acc + part
    for i, out in enumerate(outs):
        @pl.when(s == i)
        def _(out=out):
            out[...] = acc


def reduce_kernel(idx_ref, rhs_ref, a_ref, b_ref, c_ref, d_ref, out_ref):
    total = (a_ref[...] + b_ref[...]) + (c_ref[...] + d_ref[...])
    out_ref[...] = rhs_ref[...] - total.T


def solve_kernel(idx_ref, inv_ref, a_ref, b_ref, c_ref, d_ref, out_ref):
    row = idx_ref[1]
    acc = None
    for s, ref in enumerate((a_ref, b_ref, c_ref, d_ref)):
        q = ref.shape[0]
        start = pl.multiple_of(((row + s) % 4) * q, q)
        ih, il = split2(inv_ref[:, pl.ds(start, q)])
        rh, rl = split2(ref[...])
        part = dot(ih, rh) + (dot(ih, rl) + dot(il, rh))
        acc = part if acc is None else acc + part
    out_ref[...] = acc


def shards(parent_solution, border_owner, border_slot, border_tile, pivot_inverse, pivot_rhs):
    axes = ("child", "row", "col")
    n_child = lax.axis_size("child")
    n_row = lax.axis_size("row")
    n_col = lax.axis_size("col")
    n_z = n_col // 2
    devices = n_child * n_row * n_col
    me = lax.axis_index(axes)
    my_row = lax.axis_index("row")
    my_col = lax.axis_index("col")
    idx = jnp.stack([me, my_row, my_col // 2, my_col % 2]).astype(I32)
    tile = border_tile[0]
    inverse = pivot_inverse[0]
    rhs = pivot_rhs[0]
    loads = parent_solution.shape[1]
    lanes = 128
    border = border_slot.shape[1]
    block = border // (n_row * n_col)
    quarter = rhs.shape[0] // n_row
    owner = border_owner.reshape(n_child * border // lanes, lanes)
    slot = border_slot.reshape(n_child, border // lanes, lanes).transpose(1, 0, 2).reshape(
        n_child * border // lanes, lanes)

    smem = pl.BlockSpec(memory_space=pltpu.SMEM)
    vmem = pl.BlockSpec(memory_space=pltpu.VMEM)
    params = functools.partial(pltpu.CompilerParams, vmem_limit_bytes=48 << 20)

    outgoing = pl.pallas_call(
        pick_kernel,
        in_specs=[smem, vmem, vmem, vmem],
        out_specs=vmem,
        out_shape=jax.ShapeDtypeStruct((devices * 2 * SLOTS, lanes), F32),
        compiler_params=params(),
        name="pick",
    )(idx, owner, slot, parent_solution)
    received = lax.all_to_all(
        outgoing.reshape(devices, 2 * SLOTS, lanes), axes, split_axis=0, concat_axis=0, tiled=True)
    placed = pl.pallas_call(
        place_kernel,
        in_specs=[smem, vmem, vmem],
        out_specs=vmem,
        out_shape=jax.ShapeDtypeStruct((loads, block), F32),
        compiler_params=params(),
        name="place",
    )(idx, owner, received.reshape(devices * 2 * SLOTS, lanes))
    values = lax.all_gather(placed, "col", axis=0, tiled=False)

    square = jax.ShapeDtypeStruct((loads, quarter), F32)
    coupled = pl.pallas_call(
        couple_kernel,
        grid_spec=pltpu.PrefetchScalarGridSpec(
            num_scalar_prefetch=1,
            grid=(n_row,),
            in_specs=[
                pl.BlockSpec(values.shape, lambda s, i: (0, 0, 0)),
                pl.BlockSpec((tile.shape[0], quarter), lambda s, i: (0, (i[1] + 2 + s) % 4)),
            ],
            out_specs=[pl.BlockSpec((loads, quarter), lambda s, i: (0, 0))] * n_row,
        ),
        out_shape=[square] * n_row,
        compiler_params=params(dimension_semantics=("arbitrary",)),
        name="couple",
    )(idx, values, tile)

    def shift(x, axis, by):
        n = lax.axis_size(axis)
        return lax.ppermute(x, axis, [(i, (i + by) % n) for i in range(n)])

    arrived = [shift(coupled[(s + 2) % 4], "row", s) for s in (2, 1, 3)]
    reduced = pl.pallas_call(
        reduce_kernel,
        grid_spec=pltpu.PrefetchScalarGridSpec(
            num_scalar_prefetch=1,
            grid=(1,),
            in_specs=[pl.BlockSpec((quarter, loads), lambda s, i: (i[1], 0))]
            + [pl.BlockSpec((loads, quarter), lambda s, i: (0, 0))] * 4,
            out_specs=pl.BlockSpec((quarter, loads), lambda s, i: (0, 0)),
        ),
        out_shape=jax.ShapeDtypeStruct((quarter, loads), F32),
        compiler_params=params(dimension_semantics=("arbitrary",)),
        name="reduce",
    )(idx, rhs, coupled[2], *arrived)
    far, near, back = [shift(reduced, "row", n_row - s) for s in (2, 1, 3)]
    pieces = [reduced, near, far, back]

    def solve(parity):
        return pl.pallas_call(
            solve_kernel,
            grid_spec=pltpu.PrefetchScalarGridSpec(
                num_scalar_prefetch=1,
                grid=(n_z,),
                in_specs=[pl.BlockSpec(
                    (block, inverse.shape[1]),
                    lambda s, i: (2 * ((i[2] + s) % 4) + (i[3] + parity) % 2, 0))]
                + [pl.BlockSpec((quarter, loads), lambda s, i: (0, 0))] * 4,
                out_specs=pl.BlockSpec((None, block, loads), lambda s, i: (s, 0, 0)),
            ),
            out_shape=jax.ShapeDtypeStruct((n_z, block, loads), F32),
            compiler_params=params(dimension_semantics=("arbitrary",)),
            name="solve",
        )(idx, inverse, *pieces)

    other = solve(1)
    swapped = lax.ppermute(other, "col", [(i, i ^ 1) for i in range(n_col)])
    mine = solve(0)
    chip = [mine[s] + swapped[s] for s in range(n_z)]

    def shift_z(x, by):
        return lax.ppermute(
            x, "col", [(2 * z + c, 2 * ((z + by) % n_z) + c) for z in range(n_z) for c in range(2)])

    got = [shift_z(chip[s], s) for s in (2, 1, 3)]
    return ((chip[0] + got[0]) + (got[1] + got[2]))[None]


def solution(mesh):
    return jax.shard_map(
        shards,
        mesh=mesh,
        in_specs=(
            P(("child", "row", "col"), None),
            P(),
            P(),
            P("child", "row", "col"),
            P("child", "row", "col"),
            P("child", "col", None),
        ),
        out_specs=P("child", ("row", "col"), None),
        check_vma=False,
    )
```

profile of v0, /device:TPU:0, one launch (start us, length us, event | category | flops | bytes accessed | tf_op | source)
XLA Modules:
  0.0 134.8 jit_solution(7638495394316906770)
XLA Ops:
  6.5 0.0 copy-start.1
  6.5 0.0 all-gather.3.cloned.1.call-start
  6.5 0.1 pad_add_fusion.idx_ref
  6.6 0.0 copy-start.2
  6.6 1.0 copy-done.2
  7.6 0.0 copy-start.3
  7.6 0.9 copy-done.3
  8.5 0.0 copy-start.4
  8.5 0.9 copy-done.4
  9.4 1.3 pick.1
  10.7 24.7 %all_to_all.5 = f32[128,8,128]{2,1,0:T(8,128)S(1)} all-to-all(f32[128,8,128]{2,1,0:T(8,128)S(1)} %bitcast.33), channel_id=1, replica_groups=mesh['child'=4,'row'=4,'col'=8] {'child','row','col'}, dimensions={0} | all-to-all | bytes 1048576 | tf_op jit(solution)/shard_map/all_to_all | solution.py:163
  35.4 2.1 %place.1 = f32[256,256]{1,0:T(8,128)} custom-call(s32[4]{0:T(128)S(1)} %pad_add_fusion.idx_ref, s32[256,128]{1,0:T(8,128)S(1)} %bitcast.37, f32[1024,128]{1,0:T(8,128)S(1)} %bitcast.32), custom_call_target="tpu_custom_call" | custom-call | tf_op jit(solution)/shard_map/place/pallas_call | solution.py:165
  37.5 0.0 all-gather.3.cloned.1.call-update
  37.5 21.3 %all-gather.3.cloned.1.call-done = f32[2048,256]{1,0:T(8,128)} async-done(((f32[256,256]{1,0:T(8,128)}), f32[2048,256]{1,0:T(8,128)}) %all-gather.3.cloned.1.call-update) | async-done | bytes 2097168 | tf_op jit(solution)/shard_map/all_gather | solution.py:173
  58.8 0.0 copy-start
  58.8 1.6 %copy-done = f32[2048,256]{1,0:T(8,128)S(1)} copy-done((f32[2048,256]{1,0:T(8,128)S(1)}, f32[2048,256]{1,0:T(8,128)}, u32[]{:S(2)}) %copy-start) | copy-done | bytes 2097176
  60.4 7.2 %couple.1 = (f32[256,256]{1,0:T(8,128)S(1)}, f32[256,256]{1,0:T(8,128)S(1)}, f32[256,256]{1,0:T(8,128)S(1)}, f32[256,256]{1,0:T(8,128)S(1)}) custom-call(s32[4]{0:T(128)S(1)} %pad_add_fusion.idx_ref, f32[8,256,256]{2,1,0:T(8,128)S(1)} %bitcast.34, f32[2048,1024]{1,0:T(8,128)} %bitcast.41), custom_call_target="tpu_custom_call" | custom-call | tf_op jit(solution)/shard_map/couple/pallas_call | solution.py:176
  67.5 3.1 %collective-permute-start = (f32[256,256]{1,0:T(8,128)S(1)}, f32[256,256]{1,0:T(8,128)S(1)}, u32[]{:S(2)}, u32[]{:S(2)}) collective-permute-start(f32[256,256]{1,0:T(8,128)S(1)} %get-tuple-element.10), channel_id=1, source_target_pairs={{0,16},{8,24},{16,0},{24,8},{1,17},{9,25},{17,1},{25,9},{2,18},{10... | collective-permute-start | bytes 786440 | tf_op jit(solution)/shard_map/ppermute | solution.py:194
  70.6 0.6 collective-permute-start.1
  71.2 2.7 %collective-permute-start.2 = (f32[256,256]{1,0:T(8,128)S(1)}, f32[256,256]{1,0:T(8,128)S(1)}, u32[]{:S(2)}, u32[]{:S(2)}) collective-permute-start(f32[256,256]{1,0:T(8,128)S(1)} %get-tuple-element.12), channel_id=1, source_target_pairs={{0,24},{8,0},{16,8},{24,16},{1,25},{9,1},{17,9},{25,17},{2,26},{10... | collective-permute-start | bytes 786440 | tf_op jit(solution)/shard_map/ppermute | solution.py:194
  73.8 4.5 %collective-permute-done.b_ref = f32[256,256]{1,0:T(8,128)S(1)} collective-permute-done((f32[256,256]{1,0:T(8,128)S(1)}, f32[256,256]{1,0:T(8,128)S(1)}, u32[]{:S(2)}, u32[]{:S(2)}) %collective-permute-start) | collective-permute-done | bytes 262176 | tf_op jit(solution)/shard_map/ppermute | solution.py:194
  78.3 4.9 %collective-permute-done.1.c_ref = f32[256,256]{1,0:T(8,128)S(1)} collective-permute-done((f32[256,256]{1,0:T(8,128)S(1)}, f32[256,256]{1,0:T(8,128)S(1)}, u32[]{:S(2)}, u32[]{:S(2)}) %collective-permute-start.1) | collective-permute-done | bytes 262176 | tf_op jit(solution)/shard_map/ppermute | solution.py:194
  83.2 0.1 collective-permute-done.2.d_ref
  83.3 0.0 copy-done.1
  83.3 0.7 reduce.1.a_ref
  84.0 1.5 %collective-permute-start.5 = (f32[256,256]{1,0:T(8,128)S(1)}, f32[256,256]{1,0:T(8,128)S(1)}, u32[]{:S(2)}, u32[]{:S(2)}) collective-permute-start(f32[256,256]{1,0:T(8,128)S(1)} %reduce.1.a_ref), channel_id=1, source_target_pairs={{0,8},{8,16},{16,24},{24,0},{1,9},{9,17},{17,25},{25,1},{2,10},{10... | collective-permute-start | bytes 786440 | tf_op jit(solution)/shard_map/ppermute | solution.py:194
  85.5 2.6 %collective-permute-start.4 = (f32[256,256]{1,0:T(8,128)S(1)}, f32[256,256]{1,0:T(8,128)S(1)}, u32[]{:S(2)}, u32[]{:S(2)}) collective-permute-start(f32[256,256]{1,0:T(8,128)S(1)} %reduce.1.a_ref), channel_id=1, source_target_pairs={{0,16},{8,24},{16,0},{24,8},{1,17},{9,25},{17,1},{25,9},{2,18},{10... | collective-permute-start | bytes 786440 | tf_op jit(solution)/shard_map/ppermute | solution.py:194
  88.1 0.6 collective-permute-start.3
  88.7 4.7 %collective-permute-done.5.d_ref = f32[256,256]{1,0:T(8,128)S(1)} collective-permute-done((f32[256,256]{1,0:T(8,128)S(1)}, f32[256,256]{1,0:T(8,128)S(1)}, u32[]{:S(2)}, u32[]{:S(2)}) %collective-permute-start.5) | collective-permute-done | bytes 262176 | tf_op jit(solution)/shard_map/ppermute | solution.py:194
  93.4 6.5 %collective-permute-done.4.c_ref = f32[256,256]{1,0:T(8,128)S(1)} collective-permute-done((f32[256,256]{1,0:T(8,128)S(1)}, f32[256,256]{1,0:T(8,128)S(1)}, u32[]{:S(2)}, u32[]{:S(2)}) %collective-permute-start.4) | collective-permute-done | bytes 262176 | tf_op jit(solution)/shard_map/ppermute | solution.py:194
  99.9 0.0 collective-permute-done.3.b_ref
  99.9 5.1 %solve.3 = f32[4,256,256]{2,1,0:T(8,128)S(1)} custom-call(s32[4]{0:T(128)S(1)} %pad_add_fusion.idx_ref, f32[2048,1024]{1,0:T(8,128)} %bitcast.39, f32[256,256]{1,0:T(8,128)S(1)} %reduce.1.a_ref, f32[256,256]{1,0:T(8,128)S(1)} %collective-permute-done.3.b_ref, f32[256,256]{1,0:T(8,128)S(1)} %collective-permute-done.4.c_ref, ...), custom_call_target="tpu_custom_call" | custom-call | tf_op jit(solution)/shard_map/solve/pallas_call | solution.py:214
  105.0 0.1 collective-permute-start.6
  105.1 5.1 %solve.2 = f32[4,256,256]{2,1,0:T(8,128)S(1)} custom-call(s32[4]{0:T(128)S(1)} %pad_add_fusion.idx_ref, f32[2048,1024]{1,0:T(8,128)} %bitcast.40, f32[256,256]{1,0:T(8,128)S(1)} %reduce.1.a_ref, f32[256,256]{1,0:T(8,128)S(1)} %collective-permute-done.3.b_ref, f32[256,256]{1,0:T(8,128)S(1)} %collective-permute-done.4.c_ref, ...), custom_call_target="tpu_custom_call" | custom-call | tf_op jit(solution)/shard_map/solve/pallas_call | solution.py:214
  110.2 0.0 collective-permute-done.6
  110.2 0.1 fusion
  110.3 1.6 %collective-permute-start.9 = (f32[256,256]{1,0:T(8,128)S(1)}, f32[256,256]{1,0:T(8,128)S(1)}, u32[]{:S(2)}, u32[]{:S(2)}) collective-permute-start(f32[256,256]{1,0:T(8,128)S(1)} %get-tuple-element.13), channel_id=1, source_target_pairs={{0,6},{1,7},{2,0},{3,1},{4,2},{5,3},{6,4},{7,5},{8,14},{9,15},{10,... | collective-permute-start | bytes 786440 | tf_op jit(solution)/shard_map/ppermute | solution.py:236
  111.9 0.5 collective-permute-start.8
  112.4 2.2 %collective-permute-start.7 = (f32[256,256]{1,0:T(8,128)S(1)}, f32[256,256]{1,0:T(8,128)S(1)}, u32[]{:S(2)}, u32[]{:S(2)}) collective-permute-start(f32[256,256]{1,0:T(8,128)S(1)} %get-tuple-element.15), channel_id=1, source_target_pairs={{0,4},{1,5},{2,6},{3,7},{4,0},{5,1},{6,2},{7,3},{8,12},{9,13},{10,... | collective-permute-start | bytes 786440 | tf_op jit(solution)/shard_map/ppermute | solution.py:236
  114.6 4.8 %collective-permute-done.9 = f32[256,256]{1,0:T(8,128)S(1)} collective-permute-done((f32[256,256]{1,0:T(8,128)S(1)}, f32[256,256]{1,0:T(8,128)S(1)}, u32[]{:S(2)}, u32[]{:S(2)}) %collective-permute-start.9) | collective-permute-done | bytes 262176 | tf_op jit(solution)/shard_map/ppermute | solution.py:236
  119.4 7.7 %collective-permute-done.8 = f32[256,256]{1,0:T(8,128)S(1)} collective-permute-done((f32[256,256]{1,0:T(8,128)S(1)}, f32[256,256]{1,0:T(8,128)S(1)}, u32[]{:S(2)}, u32[]{:S(2)}) %collective-permute-start.8) | collective-permute-done | bytes 262176 | tf_op jit(solution)/shard_map/ppermute | solution.py:236
  127.2 0.0 collective-permute-done.7
  127.2 0.8 fusion.6
Async XLA Ops:
  6.5 76.7 %copy-start.1 = (f32[1,1024,256]{2,1,0:T(8,128)S(1)}, f32[1,1024,256]{2,1,0:T(8,128)}, u32[]{:S(2)}) copy-start(f32[1,1024,256]{2,1,0:T(8,128)} %param.11) | copy-start | bytes 3145732
  6.5 52.2 %all-gather.3.cloned.1.call-start = ((), (), s32[]{:S(2)}) async-start(), calls=%async_computation.1 | async-start | bytes 2359296 | tf_op jit(solution)/shard_map/all_gather | solution.py:173
  6.6 1.0 copy-start.2
  7.6 0.9 copy-start.3
  8.5 0.9 copy-start.4
  58.8 1.6 %copy-start = (f32[2048,256]{1,0:T(8,128)S(1)}, f32[2048,256]{1,0:T(8,128)}, u32[]{:S(2)}) copy-start(f32[2048,256]{1,0:T(8,128)} %all-gather.3.cloned.1.call-done) | copy-start | bytes 6291460
  67.5 10.8 %collective-permute-start = (f32[256,256]{1,0:T(8,128)S(1)}, f32[256,256]{1,0:T(8,128)S(1)}, u32[]{:S(2)}, u32[]{:S(2)}) collective-permute-start(f32[256,256]{1,0:T(8,128)S(1)} %get-tuple-element.10), channel_id=1, source_target_pairs={{0,16},{8,24},{16,0},{24,8},{1,17},{9,25},{17,1},{25,9},{2,18},{10... | collective-permute-start | bytes 786440 | tf_op jit(solution)/shard_map/ppermute | solution.py:194
  70.6 12.6 %collective-permute-start.1 = (f32[256,256]{1,0:T(8,128)S(1)}, f32[256,256]{1,0:T(8,128)S(1)}, u32[]{:S(2)}, u32[]{:S(2)}) collective-permute-start(f32[256,256]{1,0:T(8,128)S(1)} %get-tuple-element.11), channel_id=1, source_target_pairs={{0,8},{8,16},{16,24},{24,0},{1,9},{9,17},{17,25},{25,1},{2,10},{10... | collective-permute-start | bytes 786440 | tf_op jit(solution)/shard_map/ppermute | solution.py:194
  71.2 12.1 %collective-permute-start.2 = (f32[256,256]{1,0:T(8,128)S(1)}, f32[256,256]{1,0:T(8,128)S(1)}, u32[]{:S(2)}, u32[]{:S(2)}) collective-permute-start(f32[256,256]{1,0:T(8,128)S(1)} %get-tuple-element.12), channel_id=1, source_target_pairs={{0,24},{8,0},{16,8},{24,16},{1,25},{9,1},{17,9},{25,17},{2,26},{10... | collective-permute-start | bytes 786440 | tf_op jit(solution)/shard_map/ppermute | solution.py:194
  84.0 9.5 %collective-permute-start.5 = (f32[256,256]{1,0:T(8,128)S(1)}, f32[256,256]{1,0:T(8,128)S(1)}, u32[]{:S(2)}, u32[]{:S(2)}) collective-permute-start(f32[256,256]{1,0:T(8,128)S(1)} %reduce.1.a_ref), channel_id=1, source_target_pairs={{0,8},{8,16},{16,24},{24,0},{1,9},{9,17},{17,25},{25,1},{2,10},{10... | collective-permute-start | bytes 786440 | tf_op jit(solution)/shard_map/ppermute | solution.py:194
  85.5 14.5 %collective-permute-start.4 = (f32[256,256]{1,0:T(8,128)S(1)}, f32[256,256]{1,0:T(8,128)S(1)}, u32[]{:S(2)}, u32[]{:S(2)}) collective-permute-start(f32[256,256]{1,0:T(8,128)S(1)} %reduce.1.a_ref), channel_id=1, source_target_pairs={{0,16},{8,24},{16,0},{24,8},{1,17},{9,25},{17,1},{25,9},{2,18},{10... | collective-permute-start | bytes 786440 | tf_op jit(solution)/shard_map/ppermute | solution.py:194
  88.1 11.8 %collective-permute-start.3 = (f32[256,256]{1,0:T(8,128)S(1)}, f32[256,256]{1,0:T(8,128)S(1)}, u32[]{:S(2)}, u32[]{:S(2)}) collective-permute-start(f32[256,256]{1,0:T(8,128)S(1)} %reduce.1.a_ref), channel_id=1, source_target_pairs={{0,24},{8,0},{16,8},{24,16},{1,25},{9,1},{17,9},{25,17},{2,26},{10... | collective-permute-start | bytes 786440 | tf_op jit(solution)/shard_map/ppermute | solution.py:194
  105.0 5.2 %collective-permute-start.6 = (f32[4,256,256]{2,1,0:T(8,128)S(1)}, f32[4,256,256]{2,1,0:T(8,128)S(1)}, u32[]{:S(2)}, u32[]{:S(2)}) collective-permute-start(f32[4,256,256]{2,1,0:T(8,128)S(1)} %solve.3), channel_id=1, source_target_pairs={{0,1},{1,0},{2,3},{3,2},{4,5},{5,4},{6,7},{7,6},{8,9},{9,8},{10,11... | collective-permute-start | bytes 3145736 | tf_op jit(solution)/shard_map/ppermute | solution.py:231
  110.3 9.2 %collective-permute-start.9 = (f32[256,256]{1,0:T(8,128)S(1)}, f32[256,256]{1,0:T(8,128)S(1)}, u32[]{:S(2)}, u32[]{:S(2)}) collective-permute-start(f32[256,256]{1,0:T(8,128)S(1)} %get-tuple-element.13), channel_id=1, source_target_pairs={{0,6},{1,7},{2,0},{3,1},{4,2},{5,3},{6,4},{7,5},{8,14},{9,15},{10,... | collective-permute-start | bytes 786440 | tf_op jit(solution)/shard_map/ppermute | solution.py:236
  111.9 15.3 %collective-permute-start.8 = (f32[256,256]{1,0:T(8,128)S(1)}, f32[256,256]{1,0:T(8,128)S(1)}, u32[]{:S(2)}, u32[]{:S(2)}) collective-permute-start(f32[256,256]{1,0:T(8,128)S(1)} %get-tuple-element.14), channel_id=1, source_target_pairs={{0,2},{1,3},{2,4},{3,5},{4,6},{5,7},{6,0},{7,1},{8,10},{9,11},{10,... | collective-permute-start | bytes 786440 | tf_op jit(solution)/shard_map/ppermute | solution.py:236
  112.4 14.8 %collective-permute-start.7 = (f32[256,256]{1,0:T(8,128)S(1)}, f32[256,256]{1,0:T(8,128)S(1)}, u32[]{:S(2)}, u32[]{:S(2)}) collective-permute-start(f32[256,256]{1,0:T(8,128)S(1)} %get-tuple-element.15), channel_id=1, source_target_pairs={{0,4},{1,5},{2,6},{3,7},{4,0},{5,1},{6,2},{7,3},{8,12},{9,13},{10,... | collective-permute-start | bytes 786440 | tf_op jit(solution)/shard_map/ppermute | solution.py:236
Sparse Core Ops, SparseCore 0:
  37.6 21.1 all-gather.2
where the time goes:
time: 135 us
  waiting for transfers between devices  54.5 us (40%)
  blocking collectives  24.7 us (18%)
  Pallas kernels  21.3 us (16%)
  starting transfers between devices  15.5 us (11%)
  between operations  13.5 us (10%)
  local copies, waits for them, and re-layouts  4.38 us (3%)
    all_to_all x1, blocking collectives, shards(): lax.all_to_all(outgoing.reshape(devices, 2 * SLOTS, lanes), axes, split_a...  24.7 us
    all_gather x1, waiting for transfers between devices, shards(): values = lax.all_gather(placed, 'col', axis=0, tiled=False)  21.3 us
    ppermute x6, waiting for transfers between devices, shift(): return lax.ppermute(x, axis, [(i, (i + by) % n) for i in range(n)])  20.7 us
    ppermute x3, waiting for transfers between devices, shift_z(): lax.ppermute(x, 'col', [(2 * z + c, 2 * ((z + by) % n_z) + c) for z in ra...  12.6 us
    ppermute x6, starting transfers between devices, shift(): return lax.ppermute(x, axis, [(i, (i + by) % n) for i in range(n)])  11 us
    pallas_call x2, Pallas kernels, solve(): pl.pallas_call(solve_kernel, grid_spec=pltpu.PrefetchScalarGridSpec(num_s...  10.1 us
    pallas_call x1, Pallas kernels, shards(): pl.pallas_call(couple_kernel, grid_spec=pltpu.PrefetchScalarGridSpec(num_...  7.17 us
    unnamed x10, local copies, waits for them, and re-layouts  4.38 us
  transfers between devices with their start and end apart: 11, of which 8 were waited for; matrix products, arithmetic and copies ran while one was open for 0% of the time, Pallas kernels for 4%

commit v1 on v0

v1 whole, which is shorter than its diff:
```python
import functools

import jax
import jax.numpy as jnp
from jax import lax
from jax.experimental import pallas as pl
from jax.experimental.pallas import tpu as pltpu
from jax.sharding import PartitionSpec as P

F32 = jnp.float32
BF16 = jnp.bfloat16
I32 = jnp.int32
CHUNKS = 2
SLOTS = 4


def position():
    col = lax.axis_index("col")
    return lax.axis_index(("child", "row", "col")), lax.axis_index("row"), col // 2, col % 2


def dot(a, b):
    return jnp.dot(a, b, preferred_element_type=F32)


def split2(x):
    hi = x.astype(BF16)
    return hi, (x - hi.astype(F32)).astype(BF16)


def split3(x):
    hi = x.astype(BF16)
    rest = x - hi.astype(F32)
    mid = rest.astype(BF16)
    return hi, mid, (rest - mid.astype(F32)).astype(BF16)


def ones_upto(n):
    rows = lax.broadcasted_iota(I32, (n, n), 0)
    cols = lax.broadcasted_iota(I32, (n, n), 1)
    return jnp.where(rows <= cols, 1.0, 0.0).astype(BF16)


def indicator(flag):
    return jnp.where(flag, 1.0, 0.0).astype(BF16)


def pick_kernel(owner_hbm, slot_hbm, parent_hbm, out_ref, mine_ref,
                owner_ref, slot_ref, parent_ref, sems):
    copies = [pltpu.make_async_copy(src, dst, sems.at[n]) for n, (src, dst) in enumerate(
        [(owner_hbm, owner_ref), (slot_hbm, slot_ref), (parent_hbm, parent_ref)])]
    for copy in copies:
        copy.start()
    copies[0].wait()
    me = position()[0]
    mine_ref[...] = owner_ref[pl.ds(2 * me, 2), :]
    blocks = owner_ref.shape[0] // 2
    lanes = owner_ref.shape[1]
    upto = ones_upto(lanes)
    copies[1].wait()
    copies[2].wait()
    parts = [split3(parent_ref[:, h * lanes:(h + 1) * lanes]) for h in range(2)]
    mask = [owner_ref[pl.ds(h, blocks, stride=2), :] == me for h in range(2)]
    slot = []
    children = 4
    per_child = blocks // children
    for h in range(2):
        slot.append(jnp.concatenate(
            [slot_ref[pl.ds(children * h + c, per_child, stride=2 * children), :]
             for c in range(children)], axis=0))
    count0 = dot(indicator(mask[0]), upto)
    count1 = dot(indicator(mask[1]), upto) + count0[:, lanes - 1:lanes]
    count = [count0, count1]
    local = lax.broadcasted_iota(I32, (blocks, lanes), 1)
    for p in range(SLOTS):
        asked = jnp.zeros((blocks, 1), I32)
        for h in range(2):
            chosen = mask[h] & (count[h] == float(p + 1))
            asked = asked + jnp.sum(jnp.where(chosen, slot[h] + 1, 0), axis=1, keepdims=True)
        select = indicator(local + 1 == asked)
        for h in range(2):
            hi, mid, lo = parts[h]
            out_ref[pl.ds(2 * p + h, blocks, stride=2 * SLOTS), :] = (
                dot(select, lo) + dot(select, mid)) + dot(select, hi)


def load_kernel(order_ref, tile_hbm, tile_ref, done_ref, sems):
    del order_ref
    done_ref[...] = jnp.zeros(done_ref.shape, F32)
    parts = sems.shape[0]
    rows = tile_ref.shape[0] // parts
    copies = []
    for n in range(parts):
        part = pl.ds(n * rows, rows)
        copies.append(pltpu.make_async_copy(tile_hbm.at[part], tile_ref.at[part], sems.at[n]))
    for copy in copies:
        copy.start()
    for copy in copies:
        copy.wait()


def place_kernel(mine_ref, got_ref, *refs, half):
    out_ref = refs[-1]
    lanes = mine_ref.shape[1]
    devices = got_ref.shape[0] // (2 * SLOTS)
    upto = ones_upto(lanes)
    source = lax.broadcasted_iota(I32, (devices, lanes), 0)
    flag = [source == mine_ref[h:h + 1, :] for h in range(2)]
    count0 = dot(indicator(flag[0]), upto)
    count1 = dot(indicator(flag[1]), upto) + count0[:, lanes - 1:lanes]
    count = [count0, count1]
    acc = [jnp.zeros((lanes, lanes), F32) for _ in range(2)]
    for p in range(SLOTS):
        rows = got_ref[pl.ds(2 * p + half, devices, stride=2 * SLOTS), :]
        parts = split3(rows.T)
        for h in range(2):
            choose = indicator(flag[h] & (count[h] == float(p + 1)))
            for part in parts:
                acc[h] = acc[h] + dot(part, choose)
    for h in range(2):
        out_ref[:, h * lanes:(h + 1) * lanes] = acc[h]


def stack_kernel(a_ref, b_ref, c_ref, d_ref, order_ref, out_ref):
    del order_ref
    for n, ref in enumerate((a_ref, b_ref, c_ref, d_ref)):
        out_ref[n] = ref[...]


def couple_kernel(tile_ref, *refs):
    values, outs, split_ref = refs[:-5], refs[-5:-1], refs[-1]
    _, row, z, core = position()
    for n in range(8):
        value = values[n % 2][n // 2]
        width, rows = value.shape
        block = 2 * ((z + 4 - n // 2) % 4) + (core + n % 2) % 2
        start = pl.multiple_of(block * rows, rows)
        vh, vl = split2(value)
        split_ref[:width, pl.ds(start, rows)] = vh
        split_ref[width:, pl.ds(start, rows)] = vl
    for s, out in enumerate(outs):
        cols = out.shape[1]
        start = pl.multiple_of(((row + 2 + s) % 4) * cols, cols)
        th, tl = split2(tile_ref[:, pl.ds(start, cols)])
        both = dot(split_ref[...], th)
        out[...] = both[:width] + (both[width:] + dot(split_ref[:width], tl))


def reduce_kernel(rhs_ref, a_ref, b_ref, c_ref, d_ref, out_ref, *, chunk):
    rows, width = out_ref.shape
    start = pl.multiple_of(position()[1] * rows, rows)
    total = (a_ref[...] + b_ref[...]) + (c_ref[...] + d_ref[...])
    out_ref[...] = rhs_ref[pl.ds(start, rows), chunk * width:(chunk + 1) * width] - total.T


def product(inv_ref, split_ref, parity, s):
    rows, width = 256, split_ref.shape[1] // 2
    _, _, z, core = position()
    start = pl.multiple_of((2 * ((z + 2 + s) % 4) + (core + parity) % 2) * rows, rows)
    ih, il = split2(inv_ref[pl.ds(start, rows), :])
    both = dot(ih, split_ref[...])
    return both[:, :width] + (both[:, width:] + dot(il, split_ref[:, :width]))


def split_pieces(refs, split_ref):
    row = position()[1]
    for s, ref in enumerate(refs):
        q, width = ref.shape
        start = pl.multiple_of(((row + s) % 4) * q, q)
        rh, rl = split2(ref[...])
        split_ref[pl.ds(start, q), :width] = rh
        split_ref[pl.ds(start, q), width:] = rl


def send_kernel(inv_ref, a_ref, b_ref, c_ref, d_ref, out_ref, split_ref):
    split_pieces((a_ref, b_ref, c_ref, d_ref), split_ref)
    for s in range(4):
        out_ref[s] = product(inv_ref, split_ref, 1, s)


def keep_kernel(inv_ref, a_ref, b_ref, c_ref, d_ref, add_ref, *rest):
    outs, split_ref = rest[:-1], rest[-1]
    split_pieces((a_ref, b_ref, c_ref, d_ref), split_ref)
    for s, out in enumerate(outs):
        out[...] = product(inv_ref, split_ref, 0, s) + add_ref[s]


def shards(parent_solution, border_owner, border_slot, border_tile, pivot_inverse, pivot_rhs):
    axes = ("child", "row", "col")
    n_child = lax.axis_size("child")
    n_row = lax.axis_size("row")
    n_col = lax.axis_size("col")
    n_z = n_col // 2
    devices = n_child * n_row * n_col
    rhs = pivot_rhs[0]
    loads = parent_solution.shape[1]
    lanes = 128
    width = loads // CHUNKS
    border = border_slot.shape[1]
    block = border // (n_row * n_col)
    quarter = rhs.shape[0] // n_row
    owner = border_owner.reshape(n_child * border // lanes, lanes)
    slot = border_slot.reshape(n_child, border // lanes, lanes).transpose(1, 0, 2).reshape(
        n_child * border // lanes, lanes)
    def arr(*shape):
        return jax.ShapeDtypeStruct(shape, F32)

    def shift(x, by):
        return lax.ppermute(x, "row", [(i, (i + by) % n_row) for i in range(n_row)])

    def shift_z(x, by):
        return lax.ppermute(
            x, "col", [(2 * z + c, 2 * ((z + by) % n_z) + c) for z in range(n_z) for c in range(2)])

    def swap(x):
        return lax.ppermute(x, "col", [(i, i ^ 1) for i in range(n_col)])

    dma = pltpu.SemaphoreType.DMA
    vmem = pl.BlockSpec(memory_space=pltpu.VMEM)
    hbm = pl.BlockSpec(memory_space=pltpu.HBM)
    anywhere = pl.BlockSpec(memory_space=pl.ANY)

    def in_hbm(x):
        return pltpu.with_memory_space_constraint(x, pltpu.HBM)

    def in_vmem(x):
        return pltpu.with_memory_space_constraint(x, pltpu.VMEM)

    outgoing, mine = pl.pallas_call(
        pick_kernel,
        in_specs=[hbm, hbm, hbm],
        out_specs=[vmem, vmem],
        out_shape=[arr(devices * 2 * SLOTS, lanes), jax.ShapeDtypeStruct((2, lanes), I32)],
        scratch_shapes=[pltpu.VMEM(owner.shape, I32), pltpu.VMEM(slot.shape, I32),
                        pltpu.VMEM(parent_solution.shape, F32), dma((3,))],
        compiler_params=pltpu.CompilerParams(vmem_limit_bytes=8 << 20),
        name="pick",
    )(in_hbm(owner), in_hbm(slot), in_hbm(parent_solution))
    received = lax.all_to_all(
        outgoing.reshape(devices, 2 * SLOTS, lanes), axes, split_axis=0, concat_axis=0, tiled=True)
    received = received.reshape(devices * 2 * SLOTS, lanes)
    inverse = pivot_inverse[0]
    def place(half, *order):
        return pl.pallas_call(
            functools.partial(place_kernel, half=half),
            in_specs=[vmem, vmem] + [anywhere] * len(order),
            out_specs=vmem,
            out_shape=arr(width, block),
            compiler_params=pltpu.CompilerParams(vmem_limit_bytes=8 << 20),
            name="place",
        )(mine, received, *order)

    first = place(0)
    tile, loaded = pl.pallas_call(
        load_kernel,
        in_specs=[anywhere, hbm],
        out_specs=[vmem, vmem],
        out_shape=[pltpu.VMEM(border_tile.shape[1:], F32), arr(8, lanes)],
        scratch_shapes=[dma((4,))],
        compiler_params=pltpu.CompilerParams(vmem_limit_bytes=4 << 20),
        cost_estimate=pl.CostEstimate(
            flops=0, transcendentals=0, bytes_accessed=8 * border_tile.shape[1] * border_tile.shape[2]),
        name="load",
    )(first, in_hbm(border_tile[0]))
    placed = [first, place(1, loaded)]

    def send_z(own):
        return {s: shift_z(own, s) for s in (2, 1, 3)}

    def gather(own, got, order):
        stacked = pl.pallas_call(
            stack_kernel,
            in_specs=[vmem] * n_z + [anywhere],
            out_specs=vmem,
            out_shape=arr(n_z, width, block),
            compiler_params=pltpu.CompilerParams(vmem_limit_bytes=4 << 20),
            name="stack",
        )(own, got[1], got[2], got[3], order)
        return [stacked, swap(stacked)]

    def held(kernel, name, scratch, out_shape, *args):
        return pl.pallas_call(
            kernel,
            in_specs=[vmem] * len(args),
            out_specs=jax.tree.map(lambda _: vmem, out_shape),
            out_shape=out_shape,
            scratch_shapes=scratch,
            compiler_params=pltpu.CompilerParams(vmem_limit_bytes=8 << 20),
            name=name,
        )(*args)

    def couple(values):
        return held(couple_kernel, "couple", [pltpu.VMEM((2 * width, tile.shape[0]), BF16)],
                    [arr(width, quarter)] * n_row, in_vmem(tile), *values)

    def reduce(coupled, chunk):
        arrived = [shift(coupled[(s + 2) % 4], s) for s in (2, 1, 3)]
        return held(functools.partial(reduce_kernel, chunk=chunk), "reduce", [],
                    arr(quarter, width), rhs, coupled[2], *arrived)

    def spread(reduced):
        far, near, back = [shift(reduced, n_row - s) for s in (2, 1, 3)]
        return [reduced, near, far, back]

    def solve(pieces):
        scratch = [pltpu.VMEM((inverse.shape[1], 2 * width), BF16)]
        other = held(send_kernel, "send", scratch, arr(n_z, block, width), inverse, *pieces)
        return held(keep_kernel, "keep", scratch, [arr(block, width)] * n_z,
                    inverse, *pieces, swap(other))

    def finish(chip):
        got = [shift_z(chip[(s + 2) % 4], s) for s in (2, 1, 3)]
        return (chip[2] + got[0]) + (got[1] + got[2])

    chunks = range(CHUNKS)
    sent = [send_z(placed[c]) for c in chunks]
    coupled = [couple(gather(placed[0], sent[0], placed[1]))]
    coupled.append(couple(gather(placed[1], sent[1], coupled[0][0])))
    reduced = [reduce(coupled[c], c) for c in chunks]
    pieces = [spread(reduced[c]) for c in chunks]
    chip = [solve(pieces[c]) for c in chunks]
    return jnp.concatenate([finish(chip[c]) for c in chunks], axis=1)[None]


def solution(mesh):
    return jax.shard_map(
        shards,
        mesh=mesh,
        in_specs=(
            P(("child", "row", "col"), None),
            P(),
            P(),
            P("child", "row", "col"),
            P("child", "row", "col"),
            P("child", "col", None),
        ),
        out_specs=P("child", ("row", "col"), None),
        check_vma=False,
    )
```

time: 135 us -> 96 us (0.71)
  waiting for transfers between devices: 54.5 us -> 20.7 us
  starting transfers between devices: 15.5 us -> 31.3 us
  between operations: 13.5 us -> 0.19 us
  local copies, waits for them, and re-layouts: 4.38 us -> 0.01 us
  Pallas kernels: 21.3 us -> 17.4 us
    all_gather x1 -> x0, waiting for transfers between devices: 21.3 us -> none  [shards(): values = lax.all_gather(placed, 'col', axis=0, tiled=False)]
    ppermute x7 -> x16, waiting for transfers between devices: 20.7 us -> 8.73 us  [the longest x12 8.72 us: shift(): return lax.ppermute(x, 'row', [(i, (i + by) % n_row) for i in range(n_row)])]
    ppermute x3 -> x12, starting transfers between devices: 4.33 us -> 16 us  [shift_z(): lax.ppermute(x, 'col', [(2 * z + c, 2 * ((z + by) % n_z) + c) for z in ra...]
    unnamed x10 -> x6, local copies, waits for them, and re-layouts: 4.38 us -> 0.01 us
    ppermute x7 -> x16, starting transfers between devices: 11.1 us -> 15.3 us  [the longest x12 15 us: shift(): return lax.ppermute(x, 'row', [(i, (i + by) % n_row) for i in range(n_row)])]
    pallas_call x6 -> x14, Pallas kernels: 21.3 us -> 17.4 us  [the longest x8 10.7 us: held(): pl.pallas_call(kernel, in_specs=[vmem] * len(args), out_specs=jax.tree.ma...]
    ppermute x3 -> x12, waiting for transfers between devices: 12.6 us -> 12 us  [shift_z(): lax.ppermute(x, 'col', [(2 * z + c, 2 * ((z + by) % n_z) + c) for z in ra...]
  transfers between devices with their start and end apart: 11 -> 28, of which waited for: 8 -> 13; matrix products, arithmetic and copies ran while one was open for 0% -> 0% of each run, Pallas kernels for 4% -> 13%
where the time goes in v1:
time: 96 us; the launch traced here: 95.1 us
  starting transfers between devices  31.3 us (33%)
  blocking collectives  24.7 us (26%)
  waiting for transfers between devices  20.7 us (22%)
  Pallas kernels  17.4 us (18%)
    all_to_all x1, blocking collectives, shards(): lax.all_to_all(outgoing.reshape(devices, 2 * SLOTS, lanes), axes, split_a...  24.7 us
    ppermute x12, starting transfers between devices, shift_z(): lax.ppermute(x, 'col', [(2 * z + c, 2 * ((z + by) % n_z) + c) for z in ra...  16 us
    ppermute x12, starting transfers between devices, shift(): return lax.ppermute(x, 'row', [(i, (i + by) % n_row) for i in range(n_row)])  15 us
    ppermute x12, waiting for transfers between devices, shift_z(): lax.ppermute(x, 'col', [(2 * z + c, 2 * ((z + by) % n_z) + c) for z in ra...  12 us
    pallas_call x8, Pallas kernels, held(): pl.pallas_call(kernel, in_specs=[vmem] * len(args), out_specs=jax.tree.ma...  10.7 us
    ppermute x12, waiting for transfers between devices, shift(): return lax.ppermute(x, 'row', [(i, (i + by) % n_row) for i in range(n_row)])  8.72 us
    pallas_call x1, Pallas kernels, shards(): pl.pallas_call(load_kernel, in_specs=[anywhere, hbm], out_specs=[vmem, vm...  3.5 us
  transfers between devices with their start and end apart: 28, of which 13 were waited for; matrix products, arithmetic and copies ran while one was open for 0% of the time, Pallas kernels for 13%

profile of v1, /device:TPU:0, one launch (start us, length us, event | category | flops | bytes accessed | tf_op | source)
XLA Modules:
  0.0 95.1 jit_solution(14627124494871945661)
XLA Ops:
  0.0 1.8 %pick.1 = (f32[1024,128]{1,0:T(8,128)S(1)}, s32[2,128]{1,0:T(2,128)S(1)}) custom-call(s32[256,128]{1,0:T(8,128)} %bitcast.25, s32[256,128]{1,0:T(8,128)} %bitcast.26, f32[128,256]{1,0:T(8,128)} %parent_hbm.1), custom_call_target="tpu_custom_call" | custom-call | tf_op jit(solution)/shard_map/pick/pallas_call | solution.py:229
  1.9 24.7 %all_to_all.5 = f32[128,8,128]{2,1,0:T(8,128)S(1)} all-to-all(f32[128,8,128]{2,1,0:T(8,128)S(1)} %bitcast.23), channel_id=1, replica_groups=mesh['child'=4,'row'=4,'col'=8] {'child','row','col'}, dimensions={0} | all-to-all | bytes 1048576 | tf_op jit(solution)/shard_map/all_to_all | solution.py:239
  26.5 0.6 place.2.order_ref.a_ref
  27.1 0.3 collective-permute-start
  27.4 1.4 %collective-permute-start.1 = (f32[128,256]{1,0:T(8,128)S(1)}, f32[128,256]{1,0:T(8,128)S(1)}, u32[]{:S(2)}, u32[]{:S(2)}) collective-permute-start(f32[128,256]{1,0:T(8,128)S(1)} %place.2.order_ref.a_ref), channel_id=1, source_target_pairs={{0,4},{1,5},{2,6},{3,7},{4,0},{5,1},{6,2},{7,3},{8,12},{9,13},{10,... | collective-permute-start | bytes 393224 | tf_op jit(solution)/shard_map/ppermute | solution.py:212
  28.8 1.6 %collective-permute-start.2 = (f32[128,256]{1,0:T(8,128)S(1)}, f32[128,256]{1,0:T(8,128)S(1)}, u32[]{:S(2)}, u32[]{:S(2)}) collective-permute-start(f32[128,256]{1,0:T(8,128)S(1)} %place.2.order_ref.a_ref), channel_id=1, source_target_pairs={{0,6},{1,7},{2,0},{3,1},{4,2},{5,3},{6,4},{7,5},{8,14},{9,15},{10,... | collective-permute-start | bytes 393224 | tf_op jit(solution)/shard_map/ppermute | solution.py:212
  30.4 3.5 %load.1 = (f32[2048,1024]{1,0:T(8,128)S(1)}, f32[8,128]{1,0:T(8,128)S(1)}) custom-call(f32[128,256]{1,0:T(8,128)S(1)} %place.2.order_ref.a_ref, f32[2048,1024]{1,0:T(8,128)} %bitcast.24), custom_call_target="tpu_custom_call" | custom-call | bytes 16777216 | tf_op jit(solution)/shard_map/load/pallas_call | solution.py:254
  34.0 0.6 place.3.order_ref.a_ref
  34.6 1.5 %collective-permute-done.b_ref = f32[128,256]{1,0:T(8,128)S(1)} collective-permute-done((f32[128,256]{1,0:T(8,128)S(1)}, f32[128,256]{1,0:T(8,128)S(1)}, u32[]{:S(2)}, u32[]{:S(2)}) %collective-permute-start) | collective-permute-done | bytes 131104 | tf_op jit(solution)/shard_map/ppermute | solution.py:212
  36.1 0.4 collective-permute-done.2.d_ref
  36.6 0.8 collective-permute-start.14
  37.4 3.4 %collective-permute-start.15 = (f32[128,256]{1,0:T(8,128)S(1)}, f32[128,256]{1,0:T(8,128)S(1)}, u32[]{:S(2)}, u32[]{:S(2)}) collective-permute-start(f32[128,256]{1,0:T(8,128)S(1)} %place.3.order_ref.a_ref), channel_id=1, source_target_pairs={{0,4},{1,5},{2,6},{3,7},{4,0},{5,1},{6,2},{7,3},{8,12},{9,13},{10,... | collective-permute-start | bytes 393224 | tf_op jit(solution)/shard_map/ppermute | solution.py:212
  40.9 2.5 %couple.2 = (f32[128,256]{1,0:T(8,128)S(1)}, f32[128,256]{1,0:T(8,128)S(1)}, f32[128,256]{1,0:T(8,128)S(1)}, f32[128,256]{1,0:T(8,128)S(1)}) custom-call(f32[2048,1024]{1,0:T(8,128)S(1)} %get-tuple-element.27.tile_ref, f32[4,128,256]{2,1,0:T(8,128)S(1)} %stack.2.refs_0_, f32[4,128,256]{2,1,0:T(8,128)S(1)} %collective-permute-done.3.refs_1_), custom_call_target="tpu_custom_call" | custom-call | tf_op jit(solution)/shard_map/couple/pallas_call | solution.py:282
  43.4 0.3 collective-permute-done.14.b_ref
  43.8 3.7 %collective-permute-done.15.c_ref = f32[128,256]{1,0:T(8,128)S(1)} collective-permute-done((f32[128,256]{1,0:T(8,128)S(1)}, f32[128,256]{1,0:T(8,128)S(1)}, u32[]{:S(2)}, u32[]{:S(2)}) %collective-permute-start.15) | collective-permute-done | bytes 131104 | tf_op jit(solution)/shard_map/ppermute | solution.py:212
  47.6 1.5 %collective-permute-start.4 = (f32[128,256]{1,0:T(8,128)S(1)}, f32[128,256]{1,0:T(8,128)S(1)}, u32[]{:S(2)}, u32[]{:S(2)}) collective-permute-start(f32[128,256]{1,0:T(8,128)S(1)} %get-tuple-element.30.order_ref), channel_id=1, source_target_pairs={{0,16},{8,24},{16,0},{24,8},{1,17},{9,25},{17,1},{25,9},{2,18},{10... | collective-permute-start | bytes 393224 | tf_op jit(solution)/shard_map/ppermute | solution.py:209
  49.1 0.7 collective-permute-start.5
  49.8 2.5 %collective-permute-start.6 = (f32[128,256]{1,0:T(8,128)S(1)}, f32[128,256]{1,0:T(8,128)S(1)}, u32[]{:S(2)}, u32[]{:S(2)}) collective-permute-start(f32[128,256]{1,0:T(8,128)S(1)} %get-tuple-element.32), channel_id=1, source_target_pairs={{0,24},{8,0},{16,8},{24,16},{1,25},{9,1},{17,9},{25,17},{2,26},{10... | collective-permute-start | bytes 393224 | tf_op jit(solution)/shard_map/ppermute | solution.py:209
  52.4 2.5 %couple.3 = (f32[128,256]{1,0:T(8,128)S(1)}, f32[128,256]{1,0:T(8,128)S(1)}, f32[128,256]{1,0:T(8,128)S(1)}, f32[128,256]{1,0:T(8,128)S(1)}) custom-call(f32[2048,1024]{1,0:T(8,128)S(1)} %get-tuple-element.27.tile_ref, f32[4,128,256]{2,1,0:T(8,128)S(1)} %stack.3.refs_0_, f32[4,128,256]{2,1,0:T(8,128)S(1)} %collective-permute-done.17.refs_1_), custom_call_target="tpu_custom_call" | custom-call | tf_op jit(solution)/shard_map/couple/pallas_call | solution.py:282
  54.9 0.9 collective-permute-start.18
  55.9 0.7 collective-permute-start.19
  56.6 2.6 %collective-permute-start.20 = (f32[128,256]{1,0:T(8,128)S(1)}, f32[128,256]{1,0:T(8,128)S(1)}, u32[]{:S(2)}, u32[]{:S(2)}) collective-permute-start(f32[128,256]{1,0:T(8,128)S(1)} %get-tuple-element.40), channel_id=1, source_target_pairs={{0,24},{8,0},{16,8},{24,16},{1,25},{9,1},{17,9},{25,17},{2,26},{10... | collective-permute-start | bytes 393224 | tf_op jit(solution)/shard_map/ppermute | solution.py:209
  59.1 0.1 reduce.2.a_ref
  59.2 0.2 collective-permute-start.7
  59.4 1.6 %collective-permute-start.8 = (f32[256,128]{1,0:T(8,128)S(1)}, f32[256,128]{1,0:T(8,128)S(1)}, u32[]{:S(2)}, u32[]{:S(2)}) collective-permute-start(f32[256,128]{1,0:T(8,128)S(1)} %reduce.2.a_ref), channel_id=1, source_target_pairs={{0,16},{8,24},{16,0},{24,8},{1,17},{9,25},{17,1},{25,9},{2,18},{10... | collective-permute-start | bytes 393224 | tf_op jit(solution)/shard_map/ppermute | solution.py:209
  61.0 2.0 %collective-permute-done.18.b_ref = f32[128,256]{1,0:T(8,128)S(1)} collective-permute-done((f32[128,256]{1,0:T(8,128)S(1)}, f32[128,256]{1,0:T(8,128)S(1)}, u32[]{:S(2)}, u32[]{:S(2)}) %collective-permute-start.18) | collective-permute-done | bytes 131104 | tf_op jit(solution)/shard_map/ppermute | solution.py:209
  63.0 3.3 %collective-permute-done.19.c_ref = f32[128,256]{1,0:T(8,128)S(1)} collective-permute-done((f32[128,256]{1,0:T(8,128)S(1)}, f32[128,256]{1,0:T(8,128)S(1)}, u32[]{:S(2)}, u32[]{:S(2)}) %collective-permute-start.19) | collective-permute-done | bytes 131104 | tf_op jit(solution)/shard_map/ppermute | solution.py:209
  66.4 0.7 collective-permute-start.21
  67.0 1.6 %collective-permute-start.22 = (f32[256,128]{1,0:T(8,128)S(1)}, f32[256,128]{1,0:T(8,128)S(1)}, u32[]{:S(2)}, u32[]{:S(2)}) collective-permute-start(f32[256,128]{1,0:T(8,128)S(1)} %reduce.3.a_ref), channel_id=1, source_target_pairs={{0,16},{8,24},{16,0},{24,8},{1,17},{9,25},{17,1},{25,9},{2,18},{10... | collective-permute-start | bytes 393224 | tf_op jit(solution)/shard_map/ppermute | solution.py:209
  68.6 2.0 %collective-permute-start.23 = (f32[256,128]{1,0:T(8,128)S(1)}, f32[256,128]{1,0:T(8,128)S(1)}, u32[]{:S(2)}, u32[]{:S(2)}) collective-permute-start(f32[256,128]{1,0:T(8,128)S(1)} %reduce.3.a_ref), channel_id=1, source_target_pairs={{0,8},{8,16},{16,24},{24,0},{1,9},{9,17},{17,25},{25,1},{2,10},{10... | collective-permute-start | bytes 393224 | tf_op jit(solution)/shard_map/ppermute | solution.py:209
  70.7 1.4 %send.2 = f32[4,256,128]{2,1,0:T(8,128)S(1)} custom-call(f32[2048,1024]{1,0:T(8,128)S(1)} %bitcast.15, f32[256,128]{1,0:T(8,128)S(1)} %reduce.2.a_ref, f32[256,128]{1,0:T(8,128)S(1)} %collective-permute-done.7.b_ref, f32[256,128]{1,0:T(8,128)S(1)} %collective-permute-done.8.c_ref, f32[256,128]{1,0:T(8,128)S(1)} %collective-permute-done.9.d_ref), custom_call_target="tpu_custom_call" | custom-call | tf_op jit(solution)/shard_map/send/pallas_call | solution.py:282
  72.1 0.9 collective-permute-done.21.b_ref
  73.0 1.5 %collective-permute-done.22.c_ref = f32[256,128]{1,0:T(8,128)S(1)} collective-permute-done((f32[256,128]{1,0:T(8,128)S(1)}, f32[256,128]{1,0:T(8,128)S(1)}, u32[]{:S(2)}, u32[]{:S(2)}) %collective-permute-start.22) | collective-permute-done | bytes 131104 | tf_op jit(solution)/shard_map/ppermute | solution.py:209
  74.5 1.1 %collective-permute-done.23.d_ref = f32[256,128]{1,0:T(8,128)S(1)} collective-permute-done((f32[256,128]{1,0:T(8,128)S(1)}, f32[256,128]{1,0:T(8,128)S(1)}, u32[]{:S(2)}, u32[]{:S(2)}) %collective-permute-start.23) | collective-permute-done | bytes 131104 | tf_op jit(solution)/shard_map/ppermute | solution.py:209
  75.5 1.4 %send.3 = f32[4,256,128]{2,1,0:T(8,128)S(1)} custom-call(f32[2048,1024]{1,0:T(8,128)S(1)} %bitcast.16, f32[256,128]{1,0:T(8,128)S(1)} %reduce.3.a_ref, f32[256,128]{1,0:T(8,128)S(1)} %collective-permute-done.21.b_ref, f32[256,128]{1,0:T(8,128)S(1)} %collective-permute-done.22.c_ref, f32[256,128]{1,0:T(8,128)S(1)} %collective-permute-done.23.d_ref), custom_call_target="tpu_custom_call" | custom-call | tf_op jit(solution)/shard_map/send/pallas_call | solution.py:282
  77.0 1.4 %keep.2 = (f32[256,128]{1,0:T(8,128)S(1)}, f32[256,128]{1,0:T(8,128)S(1)}, f32[256,128]{1,0:T(8,128)S(1)}, f32[256,128]{1,0:T(8,128)S(1)}) custom-call(f32[2048,1024]{1,0:T(8,128)S(1)} %bitcast.17, f32[256,128]{1,0:T(8,128)S(1)} %reduce.2.a_ref, f32[256,128]{1,0:T(8,128)S(1)} %collective-permute-done.7.b_ref, f32[256,128]{1,0:T(8,128)S(1)} %collective-permute-done.8.c_ref, ...), custom_call_target="tpu_custom_call" | custom-call | tf_op jit(solution)/shard_map/keep/pallas_call | solution.py:282
  78.4 1.0 %collective-permute-start.11 = (f32[256,128]{1,0:T(8,128)S(1)}, f32[256,128]{1,0:T(8,128)S(1)}, u32[]{:S(2)}, u32[]{:S(2)}) collective-permute-start(f32[256,128]{1,0:T(8,128)S(1)} %get-tuple-element.34), channel_id=1, source_target_pairs={{0,4},{1,5},{2,6},{3,7},{4,0},{5,1},{6,2},{7,3},{8,12},{9,13},{10,... | collective-permute-start | bytes 393224 | tf_op jit(solution)/shard_map/ppermute | solution.py:212
  79.4 2.3 %collective-permute-start.12 = (f32[256,128]{1,0:T(8,128)S(1)}, f32[256,128]{1,0:T(8,128)S(1)}, u32[]{:S(2)}, u32[]{:S(2)}) collective-permute-start(f32[256,128]{1,0:T(8,128)S(1)} %get-tuple-element.35), channel_id=1, source_target_pairs={{0,2},{1,3},{2,4},{3,5},{4,6},{5,7},{6,0},{7,1},{8,10},{9,11},{10,... | collective-permute-start | bytes 393224 | tf_op jit(solution)/shard_map/ppermute | solution.py:212
  81.7 1.0 %collective-permute-start.13 = (f32[256,128]{1,0:T(8,128)S(1)}, f32[256,128]{1,0:T(8,128)S(1)}, u32[]{:S(2)}, u32[]{:S(2)}) collective-permute-start(f32[256,128]{1,0:T(8,128)S(1)} %get-tuple-element.36), channel_id=1, source_target_pairs={{0,6},{1,7},{2,0},{3,1},{4,2},{5,3},{6,4},{7,5},{8,14},{9,15},{10,... | collective-permute-start | bytes 393224 | tf_op jit(solution)/shard_map/ppermute | solution.py:212
  82.7 1.4 %keep.3 = (f32[256,128]{1,0:T(8,128)S(1)}, f32[256,128]{1,0:T(8,128)S(1)}, f32[256,128]{1,0:T(8,128)S(1)}, f32[256,128]{1,0:T(8,128)S(1)}) custom-call(f32[2048,1024]{1,0:T(8,128)S(1)} %bitcast.18, f32[256,128]{1,0:T(8,128)S(1)} %reduce.3.a_ref, f32[256,128]{1,0:T(8,128)S(1)} %collective-permute-done.21.b_ref, f32[256,128]{1,0:T(8,128)S(1)} %collective-permute-done.22.c_ref, ...), custom_call_target="tpu_custom_call" | custom-call | tf_op jit(solution)/shard_map/keep/pallas_call | solution.py:282
  84.0 1.4 %collective-permute-start.25 = (f32[256,128]{1,0:T(8,128)S(1)}, f32[256,128]{1,0:T(8,128)S(1)}, u32[]{:S(2)}, u32[]{:S(2)}) collective-permute-start(f32[256,128]{1,0:T(8,128)S(1)} %get-tuple-element.42), channel_id=1, source_target_pairs={{0,4},{1,5},{2,6},{3,7},{4,0},{5,1},{6,2},{7,3},{8,12},{9,13},{10,... | collective-permute-start | bytes 393224 | tf_op jit(solution)/shard_map/ppermute | solution.py:212
  85.5 0.3 collective-permute-start.26
  85.8 0.5 collective-permute-done.11
  86.3 2.4 %collective-permute-start.27 = (f32[256,128]{1,0:T(8,128)S(1)}, f32[256,128]{1,0:T(8,128)S(1)}, u32[]{:S(2)}, u32[]{:S(2)}) collective-permute-start(f32[256,128]{1,0:T(8,128)S(1)} %get-tuple-element.44), channel_id=1, source_target_pairs={{0,6},{1,7},{2,0},{3,1},{4,2},{5,3},{6,4},{7,5},{8,14},{9,15},{10,... | collective-permute-start | bytes 393224 | tf_op jit(solution)/shard_map/ppermute | solution.py:212
  88.7 0.4 collective-permute-done.12
  89.2 2.9 %collective-permute-done.25 = f32[256,128]{1,0:T(8,128)S(1)} collective-permute-done((f32[256,128]{1,0:T(8,128)S(1)}, f32[256,128]{1,0:T(8,128)S(1)}, u32[]{:S(2)}, u32[]{:S(2)}) %collective-permute-start.25) | collective-permute-done | bytes 131104 | tf_op jit(solution)/shard_map/ppermute | solution.py:212
  92.1 2.2 %collective-permute-done.26 = f32[256,128]{1,0:T(8,128)S(1)} collective-permute-done((f32[256,128]{1,0:T(8,128)S(1)}, f32[256,128]{1,0:T(8,128)S(1)}, u32[]{:S(2)}, u32[]{:S(2)}) %collective-permute-start.26) | collective-permute-done | bytes 131104 | tf_op jit(solution)/shard_map/ppermute | solution.py:212
  94.3 0.7 maximum_bitcast_fusion
  (33 shorter events, 0.6 us)
Async XLA Ops:
  27.1 8.9 %collective-permute-start = (f32[128,256]{1,0:T(8,128)S(1)}, f32[128,256]{1,0:T(8,128)S(1)}, u32[]{:S(2)}, u32[]{:S(2)}) collective-permute-start(f32[128,256]{1,0:T(8,128)S(1)} %place.2.order_ref.a_ref), channel_id=1, source_target_pairs={{0,2},{1,3},{2,4},{3,5},{4,6},{5,7},{6,0},{7,1},{8,10},{9,11},{10,... | collective-permute-start | bytes 393224 | tf_op jit(solution)/shard_map/ppermute | solution.py:212
  27.4 8.6 %collective-permute-start.1 = (f32[128,256]{1,0:T(8,128)S(1)}, f32[128,256]{1,0:T(8,128)S(1)}, u32[]{:S(2)}, u32[]{:S(2)}) collective-permute-start(f32[128,256]{1,0:T(8,128)S(1)} %place.2.order_ref.a_ref), channel_id=1, source_target_pairs={{0,4},{1,5},{2,6},{3,7},{4,0},{5,1},{6,2},{7,3},{8,12},{9,13},{10,... | collective-permute-start | bytes 393224 | tf_op jit(solution)/shard_map/ppermute | solution.py:212
  28.8 7.7 %collective-permute-start.2 = (f32[128,256]{1,0:T(8,128)S(1)}, f32[128,256]{1,0:T(8,128)S(1)}, u32[]{:S(2)}, u32[]{:S(2)}) collective-permute-start(f32[128,256]{1,0:T(8,128)S(1)} %place.2.order_ref.a_ref), channel_id=1, source_target_pairs={{0,6},{1,7},{2,0},{3,1},{4,2},{5,3},{6,4},{7,5},{8,14},{9,15},{10,... | collective-permute-start | bytes 393224 | tf_op jit(solution)/shard_map/ppermute | solution.py:212
  36.5 4.3 %collective-permute-start.3 = (f32[4,128,256]{2,1,0:T(8,128)S(1)}, f32[4,128,256]{2,1,0:T(8,128)S(1)}, u32[]{:S(2)}, u32[]{:S(2)}) collective-permute-start(f32[4,128,256]{2,1,0:T(8,128)S(1)} %stack.2.refs_0_), channel_id=1, source_target_pairs={{0,1},{1,0},{2,3},{3,2},{4,5},{5,4},{6,7},{7,6},{8,9},{9,8},{10,11... | collective-permute-start | bytes 1572872 | tf_op jit(solution)/shard_map/ppermute | solution.py:216
  36.6 7.1 %collective-permute-start.14 = (f32[128,256]{1,0:T(8,128)S(1)}, f32[128,256]{1,0:T(8,128)S(1)}, u32[]{:S(2)}, u32[]{:S(2)}) collective-permute-start(f32[128,256]{1,0:T(8,128)S(1)} %place.3.order_ref.a_ref), channel_id=1, source_target_pairs={{0,2},{1,3},{2,4},{3,5},{4,6},{5,7},{6,0},{7,1},{8,10},{9,11},{10,... | collective-permute-start | bytes 393224 | tf_op jit(solution)/shard_map/ppermute | solution.py:212
  37.4 10.1 %collective-permute-start.15 = (f32[128,256]{1,0:T(8,128)S(1)}, f32[128,256]{1,0:T(8,128)S(1)}, u32[]{:S(2)}, u32[]{:S(2)}) collective-permute-start(f32[128,256]{1,0:T(8,128)S(1)} %place.3.order_ref.a_ref), channel_id=1, source_target_pairs={{0,4},{1,5},{2,6},{3,7},{4,0},{5,1},{6,2},{7,3},{8,12},{9,13},{10,... | collective-permute-start | bytes 393224 | tf_op jit(solution)/shard_map/ppermute | solution.py:212
  40.8 6.6 %collective-permute-start.16 = (f32[128,256]{1,0:T(8,128)S(1)}, f32[128,256]{1,0:T(8,128)S(1)}, u32[]{:S(2)}, u32[]{:S(2)}) collective-permute-start(f32[128,256]{1,0:T(8,128)S(1)} %place.3.order_ref.a_ref), channel_id=1, source_target_pairs={{0,6},{1,7},{2,0},{3,1},{4,2},{5,3},{6,4},{7,5},{8,14},{9,15},{10,... | collective-permute-start | bytes 393224 | tf_op jit(solution)/shard_map/ppermute | solution.py:212
  40.8 18.3 %copy-start = (f32[1,1024,256]{2,1,0:T(8,128)S(1)}, f32[1,1024,256]{2,1,0:T(8,128)}, u32[]{:S(2)}) copy-start(f32[1,1024,256]{2,1,0:T(8,128)} %param.11) | copy-start | bytes 3145732
  40.9 29.8 %slice-start = ((s8[8388608]{0:T(1024)(128)(4,1)}), s8[4194304]{0:T(1024)(128)(4,1)S(1)}, s32[]{:S(2)}) async-start(s8[8388608]{0:T(1024)(128)(4,1)} %bitcast.13), calls=%async_computation.1 | async-start | bytes 8388608
  47.5 4.9 %collective-permute-start.17 = (f32[4,128,256]{2,1,0:T(8,128)S(1)}, f32[4,128,256]{2,1,0:T(8,128)S(1)}, u32[]{:S(2)}, u32[]{:S(2)}) collective-permute-start(f32[4,128,256]{2,1,0:T(8,128)S(1)} %stack.3.refs_0_), channel_id=1, source_target_pairs={{0,1},{1,0},{2,3},{3,2},{4,5},{5,4},{6,7},{7,6},{8,9},{9,8},{10,11... | collective-permute-start | bytes 1572872 | tf_op jit(solution)/shard_map/ppermute | solution.py:216
  47.6 9.0 %collective-permute-start.4 = (f32[128,256]{1,0:T(8,128)S(1)}, f32[128,256]{1,0:T(8,128)S(1)}, u32[]{:S(2)}, u32[]{:S(2)}) collective-permute-start(f32[128,256]{1,0:T(8,128)S(1)} %get-tuple-element.30.order_ref), channel_id=1, source_target_pairs={{0,16},{8,24},{16,0},{24,8},{1,17},{9,25},{17,1},{25,9},{2,18},{10... | collective-permute-start | bytes 393224 | tf_op jit(solution)/shard_map/ppermute | solution.py:209
  49.1 10.0 %collective-permute-start.5 = (f32[128,256]{1,0:T(8,128)S(1)}, f32[128,256]{1,0:T(8,128)S(1)}, u32[]{:S(2)}, u32[]{:S(2)}) collective-permute-start(f32[128,256]{1,0:T(8,128)S(1)} %get-tuple-element.31), channel_id=1, source_target_pairs={{0,8},{8,16},{16,24},{24,0},{1,9},{9,17},{17,25},{25,1},{2,10},{10... | collective-permute-start | bytes 393224 | tf_op jit(solution)/shard_map/ppermute | solution.py:209
  49.8 20.8 %slice-start.1 = ((s8[8388608]{0:T(1024)(128)(4,1)}), s8[4194304]{0:T(1024)(128)(4,1)S(1)}, s32[]{:S(2)}) async-start(s8[8388608]{0:T(1024)(128)(4,1)} %bitcast.13), calls=%async_computation.2 | async-start | bytes 8388608
  49.8 9.3 %collective-permute-start.6 = (f32[128,256]{1,0:T(8,128)S(1)}, f32[128,256]{1,0:T(8,128)S(1)}, u32[]{:S(2)}, u32[]{:S(2)}) collective-permute-start(f32[128,256]{1,0:T(8,128)S(1)} %get-tuple-element.32), channel_id=1, source_target_pairs={{0,24},{8,0},{16,8},{24,16},{1,25},{9,1},{17,9},{25,17},{2,26},{10... | collective-permute-start | bytes 393224 | tf_op jit(solution)/shard_map/ppermute | solution.py:209
  54.9 8.0 %collective-permute-start.18 = (f32[128,256]{1,0:T(8,128)S(1)}, f32[128,256]{1,0:T(8,128)S(1)}, u32[]{:S(2)}, u32[]{:S(2)}) collective-permute-start(f32[128,256]{1,0:T(8,128)S(1)} %get-tuple-element.38), channel_id=1, source_target_pairs={{0,16},{8,24},{16,0},{24,8},{1,17},{9,25},{17,1},{25,9},{2,18},{10... | collective-permute-start | bytes 393224 | tf_op jit(solution)/shard_map/ppermute | solution.py:209
  55.9 10.4 %collective-permute-start.19 = (f32[128,256]{1,0:T(8,128)S(1)}, f32[128,256]{1,0:T(8,128)S(1)}, u32[]{:S(2)}, u32[]{:S(2)}) collective-permute-start(f32[128,256]{1,0:T(8,128)S(1)} %get-tuple-element.39), channel_id=1, source_target_pairs={{0,8},{8,16},{16,24},{24,0},{1,9},{9,17},{17,25},{25,1},{2,10},{10... | collective-permute-start | bytes 393224 | tf_op jit(solution)/shard_map/ppermute | solution.py:209
  56.6 9.7 %collective-permute-start.20 = (f32[128,256]{1,0:T(8,128)S(1)}, f32[128,256]{1,0:T(8,128)S(1)}, u32[]{:S(2)}, u32[]{:S(2)}) collective-permute-start(f32[128,256]{1,0:T(8,128)S(1)} %get-tuple-element.40), channel_id=1, source_target_pairs={{0,24},{8,0},{16,8},{24,16},{1,25},{9,1},{17,9},{25,17},{2,26},{10... | collective-permute-start | bytes 393224 | tf_op jit(solution)/shard_map/ppermute | solution.py:209
  59.2 9.4 %collective-permute-start.7 = (f32[256,128]{1,0:T(8,128)S(1)}, f32[256,128]{1,0:T(8,128)S(1)}, u32[]{:S(2)}, u32[]{:S(2)}) collective-permute-start(f32[256,128]{1,0:T(8,128)S(1)} %reduce.2.a_ref), channel_id=1, source_target_pairs={{0,24},{8,0},{16,8},{24,16},{1,25},{9,1},{17,9},{25,17},{2,26},{10... | collective-permute-start | bytes 393224 | tf_op jit(solution)/shard_map/ppermute | solution.py:209
  59.4 11.2 %collective-permute-start.8 = (f32[256,128]{1,0:T(8,128)S(1)}, f32[256,128]{1,0:T(8,128)S(1)}, u32[]{:S(2)}, u32[]{:S(2)}) collective-permute-start(f32[256,128]{1,0:T(8,128)S(1)} %reduce.2.a_ref), channel_id=1, source_target_pairs={{0,16},{8,24},{16,0},{24,8},{1,17},{9,25},{17,1},{25,9},{2,18},{10... | collective-permute-start | bytes 393224 | tf_op jit(solution)/shard_map/ppermute | solution.py:209
  63.0 7.7 %collective-permute-start.9 = (f32[256,128]{1,0:T(8,128)S(1)}, f32[256,128]{1,0:T(8,128)S(1)}, u32[]{:S(2)}, u32[]{:S(2)}) collective-permute-start(f32[256,128]{1,0:T(8,128)S(1)} %reduce.2.a_ref), channel_id=1, source_target_pairs={{0,8},{8,16},{16,24},{24,0},{1,9},{9,17},{17,25},{25,1},{2,10},{10... | collective-permute-start | bytes 393224 | tf_op jit(solution)/shard_map/ppermute | solution.py:209
  66.4 6.6 %collective-permute-start.21 = (f32[256,128]{1,0:T(8,128)S(1)}, f32[256,128]{1,0:T(8,128)S(1)}, u32[]{:S(2)}, u32[]{:S(2)}) collective-permute-start(f32[256,128]{1,0:T(8,128)S(1)} %reduce.3.a_ref), channel_id=1, source_target_pairs={{0,24},{8,0},{16,8},{24,16},{1,25},{9,1},{17,9},{25,17},{2,26},{10... | collective-permute-start | bytes 393224 | tf_op jit(solution)/shard_map/ppermute | solution.py:209
  67.0 7.5 %collective-permute-start.22 = (f32[256,128]{1,0:T(8,128)S(1)}, f32[256,128]{1,0:T(8,128)S(1)}, u32[]{:S(2)}, u32[]{:S(2)}) collective-permute-start(f32[256,128]{1,0:T(8,128)S(1)} %reduce.3.a_ref), channel_id=1, source_target_pairs={{0,16},{8,24},{16,0},{24,8},{1,17},{9,25},{17,1},{25,9},{2,18},{10... | collective-permute-start | bytes 393224 | tf_op jit(solution)/shard_map/ppermute | solution.py:209
  68.6 6.9 %collective-permute-start.23 = (f32[256,128]{1,0:T(8,128)S(1)}, f32[256,128]{1,0:T(8,128)S(1)}, u32[]{:S(2)}, u32[]{:S(2)}) collective-permute-start(f32[256,128]{1,0:T(8,128)S(1)} %reduce.3.a_ref), channel_id=1, source_target_pairs={{0,8},{8,16},{16,24},{24,0},{1,9},{9,17},{17,25},{25,1},{2,10},{10... | collective-permute-start | bytes 393224 | tf_op jit(solution)/shard_map/ppermute | solution.py:209
  72.0 5.0 %collective-permute-start.10 = (f32[4,256,128]{2,1,0:T(8,128)S(1)}, f32[4,256,128]{2,1,0:T(8,128)S(1)}, u32[]{:S(2)}, u32[]{:S(2)}) collective-permute-start(f32[4,256,128]{2,1,0:T(8,128)S(1)} %send.2), channel_id=1, source_target_pairs={{0,1},{1,0},{2,3},{3,2},{4,5},{5,4},{6,7},{7,6},{8,9},{9,8},{10,11... | collective-permute-start | bytes 1572872 | tf_op jit(solution)/shard_map/ppermute | solution.py:216
  76.9 5.8 %collective-permute-start.24 = (f32[4,256,128]{2,1,0:T(8,128)S(1)}, f32[4,256,128]{2,1,0:T(8,128)S(1)}, u32[]{:S(2)}, u32[]{:S(2)}) collective-permute-start(f32[4,256,128]{2,1,0:T(8,128)S(1)} %send.3), channel_id=1, source_target_pairs={{0,1},{1,0},{2,3},{3,2},{4,5},{5,4},{6,7},{7,6},{8,9},{9,8},{10,11... | collective-permute-start | bytes 1572872 | tf_op jit(solution)/shard_map/ppermute | solution.py:216
  78.4 7.9 %collective-permute-start.11 = (f32[256,128]{1,0:T(8,128)S(1)}, f32[256,128]{1,0:T(8,128)S(1)}, u32[]{:S(2)}, u32[]{:S(2)}) collective-permute-start(f32[256,128]{1,0:T(8,128)S(1)} %get-tuple-element.34), channel_id=1, source_target_pairs={{0,4},{1,5},{2,6},{3,7},{4,0},{5,1},{6,2},{7,3},{8,12},{9,13},{10,... | collective-permute-start | bytes 393224 | tf_op jit(solution)/shard_map/ppermute | solution.py:212
  79.4 9.7 %collective-permute-start.12 = (f32[256,128]{1,0:T(8,128)S(1)}, f32[256,128]{1,0:T(8,128)S(1)}, u32[]{:S(2)}, u32[]{:S(2)}) collective-permute-start(f32[256,128]{1,0:T(8,128)S(1)} %get-tuple-element.35), channel_id=1, source_target_pairs={{0,2},{1,3},{2,4},{3,5},{4,6},{5,7},{6,0},{7,1},{8,10},{9,11},{10,... | collective-permute-start | bytes 393224 | tf_op jit(solution)/shard_map/ppermute | solution.py:212
  81.7 7.5 %collective-permute-start.13 = (f32[256,128]{1,0:T(8,128)S(1)}, f32[256,128]{1,0:T(8,128)S(1)}, u32[]{:S(2)}, u32[]{:S(2)}) collective-permute-start(f32[256,128]{1,0:T(8,128)S(1)} %get-tuple-element.36), channel_id=1, source_target_pairs={{0,6},{1,7},{2,0},{3,1},{4,2},{5,3},{6,4},{7,5},{8,14},{9,15},{10,... | collective-permute-start | bytes 393224 | tf_op jit(solution)/shard_map/ppermute | solution.py:212
  84.0 8.1 %collective-permute-start.25 = (f32[256,128]{1,0:T(8,128)S(1)}, f32[256,128]{1,0:T(8,128)S(1)}, u32[]{:S(2)}, u32[]{:S(2)}) collective-permute-start(f32[256,128]{1,0:T(8,128)S(1)} %get-tuple-element.42), channel_id=1, source_target_pairs={{0,4},{1,5},{2,6},{3,7},{4,0},{5,1},{6,2},{7,3},{8,12},{9,13},{10,... | collective-permute-start | bytes 393224 | tf_op jit(solution)/shard_map/ppermute | solution.py:212
  85.5 8.8 %collective-permute-start.26 = (f32[256,128]{1,0:T(8,128)S(1)}, f32[256,128]{1,0:T(8,128)S(1)}, u32[]{:S(2)}, u32[]{:S(2)}) collective-permute-start(f32[256,128]{1,0:T(8,128)S(1)} %get-tuple-element.43), channel_id=1, source_target_pairs={{0,2},{1,3},{2,4},{3,5},{4,6},{5,7},{6,0},{7,1},{8,10},{9,11},{10,... | collective-permute-start | bytes 393224 | tf_op jit(solution)/shard_map/ppermute | solution.py:212
  86.3 8.0 %collective-permute-start.27 = (f32[256,128]{1,0:T(8,128)S(1)}, f32[256,128]{1,0:T(8,128)S(1)}, u32[]{:S(2)}, u32[]{:S(2)}) collective-permute-start(f32[256,128]{1,0:T(8,128)S(1)} %get-tuple-element.44), channel_id=1, source_target_pairs={{0,6},{1,7},{2,0},{3,1},{4,2},{5,3},{6,4},{7,5},{8,14},{9,15},{10,... | collective-permute-start | bytes 393224 | tf_op jit(solution)/shard_map/ppermute | solution.py:212

commit v2 on v1

--- a/solution.py
+++ b/solution.py
@@ -99,8 +99,7 @@
         copy.wait()
 
 
-def place_kernel(mine_ref, got_ref, *refs, half):
-    out_ref = refs[-1]
+def place_kernel(mine_ref, got_ref, out_ref):
     lanes = mine_ref.shape[1]
     devices = got_ref.shape[0] // (2 * SLOTS)
     upto = ones_upto(lanes)
@@ -109,41 +108,68 @@
     count0 = dot(indicator(flag[0]), upto)
     count1 = dot(indicator(flag[1]), upto) + count0[:, lanes - 1:lanes]
     count = [count0, count1]
-    acc = [jnp.zeros((lanes, lanes), F32) for _ in range(2)]
-    for p in range(SLOTS):
-        rows = got_ref[pl.ds(2 * p + half, devices, stride=2 * SLOTS), :]
-        parts = split3(rows.T)
+    for half in range(2):
+        acc = [jnp.zeros((lanes, lanes), F32) for _ in range(2)]
+        for p in range(SLOTS):
+            rows = got_ref[pl.ds(2 * p + half, devices, stride=2 * SLOTS), :]
+            parts = split3(rows.T)
+            for h in range(2):
+                choose = indicator(flag[h] & (count[h] == float(p + 1)))
+                for part in parts:
+                    acc[h] = acc[h] + dot(part, choose)
         for h in range(2):
-            choose = indicator(flag[h] & (count[h] == float(p + 1)))
-            for part in parts:
-                acc[h] = acc[h] + dot(part, choose)
-    for h in range(2):
-        out_ref[:, h * lanes:(h + 1) * lanes] = acc[h]
-
-
-def stack_kernel(a_ref, b_ref, c_ref, d_ref, order_ref, out_ref):
+            out_ref[half * lanes:(half + 1) * lanes, h * lanes:(h + 1) * lanes] = acc[h]
+
+
+def stack_kernel(a_ref, b_ref, c_ref, d_ref, order_ref, *outs):
     del order_ref
+    width = outs[0].shape[1]
     for n, ref in enumerate((a_ref, b_ref, c_ref, d_ref)):
-        out_ref[n] = ref[...]
-
-
-def couple_kernel(tile_ref, *refs):
-    values, outs, split_ref = refs[:-5], refs[-5:-1], refs[-1]
-    _, row, z, core = position()
-    for n in range(8):
-        value = values[n % 2][n // 2]
-        width, rows = value.shape
-        block = 2 * ((z + 4 - n // 2) % 4) + (core + n % 2) % 2
-        start = pl.multiple_of(block * rows, rows)
-        vh, vl = split2(value)
-        split_ref[:width, pl.ds(start, rows)] = vh
-        split_ref[width:, pl.ds(start, rows)] = vl
+        for chunk, out in enumerate(outs):
+            out[n] = ref[chunk * width:(chunk + 1) * width, :]
+
+
+def block_rows(tile_ref, parity, first, cols, rows):
+    _, _, z, core = position()
+    parts = []
+    for s in range(4):
+        start = pl.multiple_of((2 * ((z + 4 - s) % 4) + (core + parity) % 2) * rows, rows)
+        parts.append(tile_ref[pl.ds(start, rows), pl.ds(first, cols)])
+    return jnp.concatenate(parts, axis=0)
+
+
+def split_values(ref, split_ref, top, loads):
+    n, width, rows = ref.shape
+    for s in range(n):
+        vh, vl = split2(ref[s])
+        split_ref[top:top + width, s * rows:(s + 1) * rows] = vh
+        split_ref[loads + top:loads + top + width, s * rows:(s + 1) * rows] = vl
+
+
+def begin_kernel(tile_ref, a_ref, b_ref, out_ref, split_ref):
+    width, rows = a_ref.shape[1:]
+    loads = 2 * width
+    split_values(a_ref, split_ref, 0, loads)
+    split_values(b_ref, split_ref, width, loads)
+    cols = out_ref.shape[2]
+    for q in range(out_ref.shape[0]):
+        th, tl = split2(block_rows(tile_ref, 0, q * cols, cols, rows))
+        both = dot(split_ref[...], th)
+        out_ref[q] = both[:loads] + (both[loads:] + dot(split_ref[:loads], tl))
+
+
+def couple_kernel(tile_ref, sum_ref, other_ref, *rest, chunk):
+    outs, split_ref = rest[:-1], rest[-1]
+    row = position()[1]
+    width, cols = outs[0].shape
+    rows = other_ref.shape[2]
+    split_values(other_ref, split_ref, 0, width)
     for s, out in enumerate(outs):
-        cols = out.shape[1]
-        start = pl.multiple_of(((row + 2 + s) % 4) * cols, cols)
-        th, tl = split2(tile_ref[:, pl.ds(start, cols)])
+        q = (row + 2 + s) % 4
+        th, tl = split2(block_rows(tile_ref, 1, pl.multiple_of(q * cols, cols), cols, rows))
         both = dot(split_ref[...], th)
-        out[...] = both[:width] + (both[width:] + dot(split_ref[:width], tl))
+        out[...] = sum_ref[q, chunk * width:(chunk + 1) * width, :] + (
+            both[:width] + (both[width:] + dot(split_ref[:width], tl)))
 
 
 def reduce_kernel(rhs_ref, a_ref, b_ref, c_ref, d_ref, out_ref, *, chunk):
@@ -233,24 +259,21 @@
         out_shape=[arr(devices * 2 * SLOTS, lanes), jax.ShapeDtypeStruct((2, lanes), I32)],
         scratch_shapes=[pltpu.VMEM(owner.shape, I32), pltpu.VMEM(slot.shape, I32),
                         pltpu.VMEM(parent_solution.shape, F32), dma((3,))],
-        compiler_params=pltpu.CompilerParams(vmem_limit_bytes=8 << 20),
+        compiler_params=pltpu.CompilerParams(vmem_limit_bytes=12 << 20),
         name="pick",
     )(in_hbm(owner), in_hbm(slot), in_hbm(parent_solution))
     received = lax.all_to_all(
         outgoing.reshape(devices, 2 * SLOTS, lanes), axes, split_axis=0, concat_axis=0, tiled=True)
     received = received.reshape(devices * 2 * SLOTS, lanes)
     inverse = pivot_inverse[0]
-    def place(half, *order):
-        return pl.pallas_call(
-            functools.partial(place_kernel, half=half),
-            in_specs=[vmem, vmem] + [anywhere] * len(order),
-            out_specs=vmem,
-            out_shape=arr(width, block),
-            compiler_params=pltpu.CompilerParams(vmem_limit_bytes=8 << 20),
-            name="place",
-        )(mine, received, *order)
-
-    first = place(0)
+    placed = pl.pallas_call(
+        place_kernel,
+        in_specs=[vmem, vmem],
+        out_specs=vmem,
+        out_shape=arr(loads, block),
+        compiler_params=pltpu.CompilerParams(vmem_limit_bytes=12 << 20),
+        name="place",
+    )(mine, received)
     tile, loaded = pl.pallas_call(
         load_kernel,
         in_specs=[anywhere, hbm],
@@ -261,22 +284,9 @@
         cost_estimate=pl.CostEstimate(
             flops=0, transcendentals=0, bytes_accessed=8 * border_tile.shape[1] * border_tile.shape[2]),
         name="load",
-    )(first, in_hbm(border_tile[0]))
-    placed = [first, place(1, loaded)]
-
+    )(placed, in_hbm(border_tile[0]))
     def send_z(own):
         return {s: shift_z(own, s) for s in (2, 1, 3)}
-
-    def gather(own, got, order):
-        stacked = pl.pallas_call(
-            stack_kernel,
-            in_specs=[vmem] * n_z + [anywhere],
-            out_specs=vmem,
-            out_shape=arr(n_z, width, block),
-            compiler_params=pltpu.CompilerParams(vmem_limit_bytes=4 << 20),
-            name="stack",
-        )(own, got[1], got[2], got[3], order)
-        return [stacked, swap(stacked)]
 
     def held(kernel, name, scratch, out_shape, *args):
         return pl.pallas_call(
@@ -285,13 +295,28 @@
             out_specs=jax.tree.map(lambda _: vmem, out_shape),
             out_shape=out_shape,
             scratch_shapes=scratch,
-            compiler_params=pltpu.CompilerParams(vmem_limit_bytes=8 << 20),
+            compiler_params=pltpu.CompilerParams(vmem_limit_bytes=12 << 20),
             name=name,
         )(*args)
 
-    def couple(values):
-        return held(couple_kernel, "couple", [pltpu.VMEM((2 * width, tile.shape[0]), BF16)],
-                    [arr(width, quarter)] * n_row, in_vmem(tile), *values)
+    def stack(got):
+        return pl.pallas_call(
+            stack_kernel,
+            in_specs=[vmem] * n_z + [anywhere],
+            out_specs=[vmem] * CHUNKS,
+            out_shape=[arr(n_z, width, block)] * CHUNKS,
+            compiler_params=pltpu.CompilerParams(vmem_limit_bytes=4 << 20),
+            name="stack",
+        )(placed, got[1], got[2], got[3], loaded)
+
+    def begin(stacked):
+        return held(begin_kernel, "begin", [pltpu.VMEM((2 * loads, n_z * block), BF16)],
+                    arr(n_row, loads, quarter), in_vmem(tile), *stacked)
+
+    def couple(begun, other, chunk):
+        return held(functools.partial(couple_kernel, chunk=chunk), "couple",
+                    [pltpu.VMEM((2 * width, n_z * block), BF16)],
+                    [arr(width, quarter)] * n_row, in_vmem(tile), begun, other)
 
     def reduce(coupled, chunk):
         arrived = [shift(coupled[(s + 2) % 4], s) for s in (2, 1, 3)]
@@ -313,9 +338,10 @@
         return (chip[2] + got[0]) + (got[1] + got[2])
 
     chunks = range(CHUNKS)
-    sent = [send_z(placed[c]) for c in chunks]
-    coupled = [couple(gather(placed[0], sent[0], placed[1]))]
-    coupled.append(couple(gather(placed[1], sent[1], coupled[0][0])))
+    stacked = stack(send_z(placed))
+    others = [swap(x) for x in stacked]
+    begun = begin(stacked)
+    coupled = [couple(begun, others[c], c) for c in chunks]
     reduced = [reduce(coupled[c], c) for c in chunks]
     pieces = [spread(reduced[c]) for c in chunks]
     chip = [solve(pieces[c]) for c in chunks]

time: 96 us -> 93.8 us (0.977)
  starting transfers between devices: 31.3 us -> 28.4 us
  waiting for transfers between devices: 20.7 us -> 22.8 us
  Pallas kernels: 17.4 us -> 16 us
    ppermute x12 -> x9, starting transfers between devices: 16 us -> 10.5 us  [shift_z(): lax.ppermute(x, 'col', [(2 * z + c, 2 * ((z + by) % n_z) + c) for z in ra...]
    ppermute x12 -> x9, waiting for transfers between devices: 12 us -> 16 us  [shift_z(): lax.ppermute(x, 'col', [(2 * z + c, 2 * ((z + by) % n_z) + c) for z in ra...]
    ppermute x12, starting transfers between devices: 15 us -> 17.1 us  [shift(): return lax.ppermute(x, 'row', [(i, (i + by) % n_row) for i in range(n_row)])]
    ppermute x12, waiting for transfers between devices: 8.72 us -> 6.79 us  [shift(): return lax.ppermute(x, 'row', [(i, (i + by) % n_row) for i in range(n_row)])]
    pallas_call x8 -> x9, Pallas kernels: 10.7 us -> 9.78 us  [held(): pl.pallas_call(kernel, in_specs=[vmem] * len(args), out_specs=jax.tree.ma...]
  transfers between devices with their start and end apart: 28 -> 25, of which waited for: 13 -> 13; matrix products, arithmetic and copies ran while one was open for 0% -> 0% of each run, Pallas kernels for 13% -> 11%
where the time goes in v2:
time: 93.8 us; the launch traced here: 92.8 us
  starting transfers between devices  28.4 us (30%)
  blocking collectives  24.7 us (26%)
  waiting for transfers between devices  22.8 us (24%)
  Pallas kernels  16 us (17%)
    all_to_all x1, blocking collectives, shards(): lax.all_to_all(outgoing.reshape(devices, 2 * SLOTS, lanes), axes, split_a...  24.7 us
    ppermute x12, starting transfers between devices, shift(): return lax.ppermute(x, 'row', [(i, (i + by) % n_row) for i in range(n_row)])  17.1 us
    ppermute x9, waiting for transfers between devices, shift_z(): lax.ppermute(x, 'col', [(2 * z + c, 2 * ((z + by) % n_z) + c) for z in ra...  16 us
    ppermute x9, starting transfers between devices, shift_z(): lax.ppermute(x, 'col', [(2 * z + c, 2 * ((z + by) % n_z) + c) for z in ra...  10.5 us
    pallas_call x9, Pallas kernels, held(): pl.pallas_call(kernel, in_specs=[vmem] * len(args), out_specs=jax.tree.ma...  9.78 us
    ppermute x12, waiting for transfers between devices, shift(): return lax.ppermute(x, 'row', [(i, (i + by) % n_row) for i in range(n_row)])  6.79 us
    pallas_call x1, Pallas kernels, shards(): pl.pallas_call(load_kernel, in_specs=[anywhere, hbm], out_specs=[vmem, vm...  3.5 us
  transfers between devices with their start and end apart: 25, of which 13 were waited for; matrix products, arithmetic and copies ran while one was open for 0% of the time, Pallas kernels for 11%

profile of v2, /device:TPU:0, one launch (start us, length us, event | category | flops | bytes accessed | tf_op | source)
XLA Modules:
  0.0 92.8 jit_solution(1806750939395328522)
XLA Ops:
  0.0 1.8 %pick.1 = (f32[1024,128]{1,0:T(8,128)S(1)}, s32[2,128]{1,0:T(2,128)S(1)}) custom-call(s32[256,128]{1,0:T(8,128)} %bitcast.24, s32[256,128]{1,0:T(8,128)} %bitcast.25, f32[128,256]{1,0:T(8,128)} %parent_hbm.1), custom_call_target="tpu_custom_call" | custom-call | tf_op jit(solution)/shard_map/pick/pallas_call | solution.py:255
  1.9 24.7 %all_to_all.5 = f32[128,8,128]{2,1,0:T(8,128)S(1)} all-to-all(f32[128,8,128]{2,1,0:T(8,128)S(1)} %bitcast.22), channel_id=1, replica_groups=mesh['child'=4,'row'=4,'col'=8] {'child','row','col'}, dimensions={0} | all-to-all | bytes 1048576 | tf_op jit(solution)/shard_map/all_to_all | solution.py:265
  26.5 0.8 place.1.order_ref.a_ref
  27.3 0.2 collective-permute-start.2
  27.6 2.1 %collective-permute-start.1 = (f32[256,256]{1,0:T(8,128)S(1)}, f32[256,256]{1,0:T(8,128)S(1)}, u32[]{:S(2)}, u32[]{:S(2)}) collective-permute-start(f32[256,256]{1,0:T(8,128)S(1)} %place.1.order_ref.a_ref), channel_id=1, source_target_pairs={{0,4},{1,5},{2,6},{3,7},{4,0},{5,1},{6,2},{7,3},{8,12},{9,13},{10,... | collective-permute-start | bytes 786440 | tf_op jit(solution)/shard_map/ppermute | solution.py:238
  29.7 3.5 %load.1 = (f32[2048,1024]{1,0:T(8,128)S(1)}, f32[8,128]{1,0:T(8,128)S(1)}) custom-call(f32[256,256]{1,0:T(8,128)S(1)} %place.1.order_ref.a_ref, f32[2048,1024]{1,0:T(8,128)} %bitcast.23), custom_call_target="tpu_custom_call" | custom-call | bytes 16777216 | tf_op jit(solution)/shard_map/load/pallas_call | solution.py:277
  33.2 3.4 %collective-permute-done.2.d_ref = f32[256,256]{1,0:T(8,128)S(1)} collective-permute-done((f32[256,256]{1,0:T(8,128)S(1)}, f32[256,256]{1,0:T(8,128)S(1)}, u32[]{:S(2)}, u32[]{:S(2)}) %collective-permute-start.2) | collective-permute-done | bytes 262176 | tf_op jit(solution)/shard_map/ppermute | solution.py:238
  36.7 1.6 %collective-permute-done.1.c_ref = f32[256,256]{1,0:T(8,128)S(1)} collective-permute-done((f32[256,256]{1,0:T(8,128)S(1)}, f32[256,256]{1,0:T(8,128)S(1)}, u32[]{:S(2)}, u32[]{:S(2)}) %collective-permute-start.1) | collective-permute-done | bytes 262176 | tf_op jit(solution)/shard_map/ppermute | solution.py:238
  38.3 4.6 %collective-permute-done.b_ref = f32[256,256]{1,0:T(8,128)S(1)} collective-permute-done((f32[256,256]{1,0:T(8,128)S(1)}, f32[256,256]{1,0:T(8,128)S(1)}, u32[]{:S(2)}, u32[]{:S(2)}) %collective-permute-start) | collective-permute-done | bytes 262176 | tf_op jit(solution)/shard_map/ppermute | solution.py:238
  42.9 0.1 collective-permute-start.14
  43.0 0.5 collective-permute-start.3
  43.5 1.8 %begin.1.sum_ref = f32[4,256,256]{2,1,0:T(8,128)S(1)} custom-call(f32[2048,1024]{1,0:T(8,128)S(1)} %get-tuple-element.29.tile_ref, f32[4,128,256]{2,1,0:T(8,128)S(1)} %get-tuple-element.31.a_ref, f32[4,128,256]{2,1,0:T(8,128)S(1)} %get-tuple-element.32.b_ref), custom_call_target="tpu_custom_call" | custom-call | tf_op jit(solution)/shard_map/begin/pallas_call | solution.py:292
  45.4 1.2 %couple.3 = (f32[128,256]{1,0:T(8,128)S(1)}, f32[128,256]{1,0:T(8,128)S(1)}, f32[128,256]{1,0:T(8,128)S(1)}, f32[128,256]{1,0:T(8,128)S(1)}) custom-call(f32[2048,1024]{1,0:T(8,128)S(1)} %get-tuple-element.29.tile_ref, f32[4,256,256]{2,1,0:T(8,128)S(1)} %begin.1.sum_ref, f32[4,128,256]{2,1,0:T(8,128)S(1)} %collective-permute-done.14.other_ref), custom_call_target="tpu_custom_call" | custom-call | tf_op jit(solution)/shard_map/couple/pallas_call | solution.py:292
  46.5 1.4 %collective-permute-start.15 = (f32[128,256]{1,0:T(8,128)S(1)}, f32[128,256]{1,0:T(8,128)S(1)}, u32[]{:S(2)}, u32[]{:S(2)}) collective-permute-start(f32[128,256]{1,0:T(8,128)S(1)} %get-tuple-element.42), channel_id=1, source_target_pairs={{0,16},{8,24},{16,0},{24,8},{1,17},{9,25},{17,1},{25,9},{2,18},{10... | collective-permute-start | bytes 393224 | tf_op jit(solution)/shard_map/ppermute | solution.py:235
  47.9 0.4 collective-permute-start.16
  48.4 2.8 %collective-permute-start.17 = (f32[128,256]{1,0:T(8,128)S(1)}, f32[128,256]{1,0:T(8,128)S(1)}, u32[]{:S(2)}, u32[]{:S(2)}) collective-permute-start(f32[128,256]{1,0:T(8,128)S(1)} %get-tuple-element.44), channel_id=1, source_target_pairs={{0,24},{8,0},{16,8},{24,16},{1,25},{9,1},{17,9},{25,17},{2,26},{10... | collective-permute-start | bytes 393224 | tf_op jit(solution)/shard_map/ppermute | solution.py:235
  51.2 1.2 %couple.2 = (f32[128,256]{1,0:T(8,128)S(1)}, f32[128,256]{1,0:T(8,128)S(1)}, f32[128,256]{1,0:T(8,128)S(1)}, f32[128,256]{1,0:T(8,128)S(1)}) custom-call(f32[2048,1024]{1,0:T(8,128)S(1)} %get-tuple-element.29.tile_ref, f32[4,256,256]{2,1,0:T(8,128)S(1)} %begin.1.sum_ref, f32[4,128,256]{2,1,0:T(8,128)S(1)} %collective-permute-done.3.other_ref), custom_call_target="tpu_custom_call" | custom-call | tf_op jit(solution)/shard_map/couple/pallas_call | solution.py:292
  52.3 1.1 %collective-permute-start.4 = (f32[128,256]{1,0:T(8,128)S(1)}, f32[128,256]{1,0:T(8,128)S(1)}, u32[]{:S(2)}, u32[]{:S(2)}) collective-permute-start(f32[128,256]{1,0:T(8,128)S(1)} %get-tuple-element.34), channel_id=1, source_target_pairs={{0,16},{8,24},{16,0},{24,8},{1,17},{9,25},{17,1},{25,9},{2,18},{10... | collective-permute-start | bytes 393224 | tf_op jit(solution)/shard_map/ppermute | solution.py:235
  53.4 0.5 collective-permute-start.5
  54.0 0.5 collective-permute-done.15.b_ref
  54.5 2.2 %collective-permute-start.6 = (f32[128,256]{1,0:T(8,128)S(1)}, f32[128,256]{1,0:T(8,128)S(1)}, u32[]{:S(2)}, u32[]{:S(2)}) collective-permute-start(f32[128,256]{1,0:T(8,128)S(1)} %get-tuple-element.36), channel_id=1, source_target_pairs={{0,24},{8,0},{16,8},{24,16},{1,25},{9,1},{17,9},{25,17},{2,26},{10... | collective-permute-start | bytes 393224 | tf_op jit(solution)/shard_map/ppermute | solution.py:235
  56.7 0.5 collective-permute-done.16.c_ref
  57.2 0.1 reduce.3.a_ref
  57.3 2.2 %collective-permute-start.20 = (f32[256,128]{1,0:T(8,128)S(1)}, f32[256,128]{1,0:T(8,128)S(1)}, u32[]{:S(2)}, u32[]{:S(2)}) collective-permute-start(f32[256,128]{1,0:T(8,128)S(1)} %reduce.3.a_ref), channel_id=1, source_target_pairs={{0,8},{8,16},{16,24},{24,0},{1,9},{9,17},{17,25},{25,1},{2,10},{10... | collective-permute-start | bytes 393224 | tf_op jit(solution)/shard_map/ppermute | solution.py:235
  59.4 2.8 %collective-permute-start.19 = (f32[256,128]{1,0:T(8,128)S(1)}, f32[256,128]{1,0:T(8,128)S(1)}, u32[]{:S(2)}, u32[]{:S(2)}) collective-permute-start(f32[256,128]{1,0:T(8,128)S(1)} %reduce.3.a_ref), channel_id=1, source_target_pairs={{0,16},{8,24},{16,0},{24,8},{1,17},{9,25},{17,1},{25,9},{2,18},{10... | collective-permute-start | bytes 393224 | tf_op jit(solution)/shard_map/ppermute | solution.py:235
  62.2 0.1 reduce.2.a_ref
  62.3 2.1 %collective-permute-start.9 = (f32[256,128]{1,0:T(8,128)S(1)}, f32[256,128]{1,0:T(8,128)S(1)}, u32[]{:S(2)}, u32[]{:S(2)}) collective-permute-start(f32[256,128]{1,0:T(8,128)S(1)} %reduce.2.a_ref), channel_id=1, source_target_pairs={{0,8},{8,16},{16,24},{24,0},{1,9},{9,17},{17,25},{25,1},{2,10},{10... | collective-permute-start | bytes 393224 | tf_op jit(solution)/shard_map/ppermute | solution.py:235
  64.4 1.0 %collective-permute-start.8 = (f32[256,128]{1,0:T(8,128)S(1)}, f32[256,128]{1,0:T(8,128)S(1)}, u32[]{:S(2)}, u32[]{:S(2)}) collective-permute-start(f32[256,128]{1,0:T(8,128)S(1)} %reduce.2.a_ref), channel_id=1, source_target_pairs={{0,16},{8,24},{16,0},{24,8},{1,17},{9,25},{17,1},{25,9},{2,18},{10... | collective-permute-start | bytes 393224 | tf_op jit(solution)/shard_map/ppermute | solution.py:235
  65.4 1.1 %collective-permute-done.20.d_ref = f32[256,128]{1,0:T(8,128)S(1)} collective-permute-done((f32[256,128]{1,0:T(8,128)S(1)}, f32[256,128]{1,0:T(8,128)S(1)}, u32[]{:S(2)}, u32[]{:S(2)}) %collective-permute-start.20) | collective-permute-done | bytes 131104 | tf_op jit(solution)/shard_map/ppermute | solution.py:235
  66.5 0.7 collective-permute-start.7
  67.2 2.3 %collective-permute-done.19.c_ref = f32[256,128]{1,0:T(8,128)S(1)} collective-permute-done((f32[256,128]{1,0:T(8,128)S(1)}, f32[256,128]{1,0:T(8,128)S(1)}, u32[]{:S(2)}, u32[]{:S(2)}) %collective-permute-start.19) | collective-permute-done | bytes 131104 | tf_op jit(solution)/shard_map/ppermute | solution.py:235
  69.5 1.4 %send.3 = f32[4,256,128]{2,1,0:T(8,128)S(1)} custom-call(f32[2048,1024]{1,0:T(8,128)S(1)} %bitcast.15, f32[256,128]{1,0:T(8,128)S(1)} %reduce.3.a_ref, f32[256,128]{1,0:T(8,128)S(1)} %collective-permute-done.18.b_ref, f32[256,128]{1,0:T(8,128)S(1)} %collective-permute-done.19.c_ref, f32[256,128]{1,0:T(8,128)S(1)} %collective-permute-done.20.d_ref), custom_call_target="tpu_custom_call" | custom-call | tf_op jit(solution)/shard_map/send/pallas_call | solution.py:292
  70.8 0.1 collective-permute-start.21
  70.9 1.0 %collective-permute-done.9.d_ref = f32[256,128]{1,0:T(8,128)S(1)} collective-permute-done((f32[256,128]{1,0:T(8,128)S(1)}, f32[256,128]{1,0:T(8,128)S(1)}, u32[]{:S(2)}, u32[]{:S(2)}) %collective-permute-start.9) | collective-permute-done | bytes 131104 | tf_op jit(solution)/shard_map/ppermute | solution.py:235
  71.9 1.4 %collective-permute-done.8.c_ref = f32[256,128]{1,0:T(8,128)S(1)} collective-permute-done((f32[256,128]{1,0:T(8,128)S(1)}, f32[256,128]{1,0:T(8,128)S(1)}, u32[]{:S(2)}, u32[]{:S(2)}) %collective-permute-start.8) | collective-permute-done | bytes 131104 | tf_op jit(solution)/shard_map/ppermute | solution.py:235
  73.3 1.4 %send.2 = f32[4,256,128]{2,1,0:T(8,128)S(1)} custom-call(f32[2048,1024]{1,0:T(8,128)S(1)} %bitcast.16, f32[256,128]{1,0:T(8,128)S(1)} %reduce.2.a_ref, f32[256,128]{1,0:T(8,128)S(1)} %collective-permute-done.7.b_ref, f32[256,128]{1,0:T(8,128)S(1)} %collective-permute-done.8.c_ref, f32[256,128]{1,0:T(8,128)S(1)} %collective-permute-done.9.d_ref), custom_call_target="tpu_custom_call" | custom-call | tf_op jit(solution)/shard_map/send/pallas_call | solution.py:292
  74.8 1.4 %keep.3 = (f32[256,128]{1,0:T(8,128)S(1)}, f32[256,128]{1,0:T(8,128)S(1)}, f32[256,128]{1,0:T(8,128)S(1)}, f32[256,128]{1,0:T(8,128)S(1)}) custom-call(f32[2048,1024]{1,0:T(8,128)S(1)} %bitcast.17, f32[256,128]{1,0:T(8,128)S(1)} %reduce.3.a_ref, f32[256,128]{1,0:T(8,128)S(1)} %collective-permute-done.18.b_ref, f32[256,128]{1,0:T(8,128)S(1)} %collective-permute-done.19.c_ref, ...), custom_call_target="tpu_custom_call" | custom-call | tf_op jit(solution)/shard_map/keep/pallas_call | solution.py:292
  76.2 1.1 %collective-permute-start.22 = (f32[256,128]{1,0:T(8,128)S(1)}, f32[256,128]{1,0:T(8,128)S(1)}, u32[]{:S(2)}, u32[]{:S(2)}) collective-permute-start(f32[256,128]{1,0:T(8,128)S(1)} %get-tuple-element.46), channel_id=1, source_target_pairs={{0,4},{1,5},{2,6},{3,7},{4,0},{5,1},{6,2},{7,3},{8,12},{9,13},{10,... | collective-permute-start | bytes 393224 | tf_op jit(solution)/shard_map/ppermute | solution.py:238
  77.3 0.4 collective-permute-start.23
  77.7 2.8 %collective-permute-start.24 = (f32[256,128]{1,0:T(8,128)S(1)}, f32[256,128]{1,0:T(8,128)S(1)}, u32[]{:S(2)}, u32[]{:S(2)}) collective-permute-start(f32[256,128]{1,0:T(8,128)S(1)} %get-tuple-element.48), channel_id=1, source_target_pairs={{0,6},{1,7},{2,0},{3,1},{4,2},{5,3},{6,4},{7,5},{8,14},{9,15},{10,... | collective-permute-start | bytes 393224 | tf_op jit(solution)/shard_map/ppermute | solution.py:238
  80.6 1.4 %keep.2 = (f32[256,128]{1,0:T(8,128)S(1)}, f32[256,128]{1,0:T(8,128)S(1)}, f32[256,128]{1,0:T(8,128)S(1)}, f32[256,128]{1,0:T(8,128)S(1)}) custom-call(f32[2048,1024]{1,0:T(8,128)S(1)} %bitcast.18, f32[256,128]{1,0:T(8,128)S(1)} %reduce.2.a_ref, f32[256,128]{1,0:T(8,128)S(1)} %collective-permute-done.7.b_ref, f32[256,128]{1,0:T(8,128)S(1)} %collective-permute-done.8.c_ref, ...), custom_call_target="tpu_custom_call" | custom-call | tf_op jit(solution)/shard_map/keep/pallas_call | solution.py:292
  81.9 1.3 %collective-permute-start.11 = (f32[256,128]{1,0:T(8,128)S(1)}, f32[256,128]{1,0:T(8,128)S(1)}, u32[]{:S(2)}, u32[]{:S(2)}) collective-permute-start(f32[256,128]{1,0:T(8,128)S(1)} %get-tuple-element.38), channel_id=1, source_target_pairs={{0,4},{1,5},{2,6},{3,7},{4,0},{5,1},{6,2},{7,3},{8,12},{9,13},{10,... | collective-permute-start | bytes 393224 | tf_op jit(solution)/shard_map/ppermute | solution.py:238
  83.3 0.8 collective-permute-done.22
  84.1 2.4 %collective-permute-start.13 = (f32[256,128]{1,0:T(8,128)S(1)}, f32[256,128]{1,0:T(8,128)S(1)}, u32[]{:S(2)}, u32[]{:S(2)}) collective-permute-start(f32[256,128]{1,0:T(8,128)S(1)} %get-tuple-element.40), channel_id=1, source_target_pairs={{0,6},{1,7},{2,0},{3,1},{4,2},{5,3},{6,4},{7,5},{8,14},{9,15},{10,... | collective-permute-start | bytes 393224 | tf_op jit(solution)/shard_map/ppermute | solution.py:238
  86.5 0.4 collective-permute-done.23
  87.0 3.0 %collective-permute-done.11 = f32[256,128]{1,0:T(8,128)S(1)} collective-permute-done((f32[256,128]{1,0:T(8,128)S(1)}, f32[256,128]{1,0:T(8,128)S(1)}, u32[]{:S(2)}, u32[]{:S(2)}) %collective-permute-start.11) | collective-permute-done | bytes 131104 | tf_op jit(solution)/shard_map/ppermute | solution.py:238
  90.0 2.1 %collective-permute-done.12 = f32[256,128]{1,0:T(8,128)S(1)} collective-permute-done((f32[256,128]{1,0:T(8,128)S(1)}, f32[256,128]{1,0:T(8,128)S(1)}, u32[]{:S(2)}, u32[]{:S(2)}) %collective-permute-start.12) | collective-permute-done | bytes 131104 | tf_op jit(solution)/shard_map/ppermute | solution.py:238
  92.1 0.7 maximum_bitcast_fusion
  (26 shorter events, 0.3 us)
Async XLA Ops:
  27.3 9.3 %collective-permute-start.2 = (f32[256,256]{1,0:T(8,128)S(1)}, f32[256,256]{1,0:T(8,128)S(1)}, u32[]{:S(2)}, u32[]{:S(2)}) collective-permute-start(f32[256,256]{1,0:T(8,128)S(1)} %place.1.order_ref.a_ref), channel_id=1, source_target_pairs={{0,6},{1,7},{2,0},{3,1},{4,2},{5,3},{6,4},{7,5},{8,14},{9,15},{10,... | collective-permute-start | bytes 786440 | tf_op jit(solution)/shard_map/ppermute | solution.py:238
  27.6 10.7 %collective-permute-start.1 = (f32[256,256]{1,0:T(8,128)S(1)}, f32[256,256]{1,0:T(8,128)S(1)}, u32[]{:S(2)}, u32[]{:S(2)}) collective-permute-start(f32[256,256]{1,0:T(8,128)S(1)} %place.1.order_ref.a_ref), channel_id=1, source_target_pairs={{0,4},{1,5},{2,6},{3,7},{4,0},{5,1},{6,2},{7,3},{8,12},{9,13},{10,... | collective-permute-start | bytes 786440 | tf_op jit(solution)/shard_map/ppermute | solution.py:238
  29.7 13.2 %collective-permute-start = (f32[256,256]{1,0:T(8,128)S(1)}, f32[256,256]{1,0:T(8,128)S(1)}, u32[]{:S(2)}, u32[]{:S(2)}) collective-permute-start(f32[256,256]{1,0:T(8,128)S(1)} %place.1.order_ref.a_ref), channel_id=1, source_target_pairs={{0,2},{1,3},{2,4},{3,5},{4,6},{5,7},{6,0},{7,1},{8,10},{9,11},{10,... | collective-permute-start | bytes 786440 | tf_op jit(solution)/shard_map/ppermute | solution.py:238
  42.9 2.4 %collective-permute-start.14 = (f32[4,128,256]{2,1,0:T(8,128)S(1)}, f32[4,128,256]{2,1,0:T(8,128)S(1)}, u32[]{:S(2)}, u32[]{:S(2)}) collective-permute-start(f32[4,128,256]{2,1,0:T(8,128)S(1)} %get-tuple-element.32.b_ref), channel_id=1, source_target_pairs={{0,1},{1,0},{2,3},{3,2},{4,5},{5,4},{6,7},{7,6},{8,9},{9,8},{10,11... | collective-permute-start | bytes 1572872 | tf_op jit(solution)/shard_map/ppermute | solution.py:242
  43.0 8.1 %collective-permute-start.3 = (f32[4,128,256]{2,1,0:T(8,128)S(1)}, f32[4,128,256]{2,1,0:T(8,128)S(1)}, u32[]{:S(2)}, u32[]{:S(2)}) collective-permute-start(f32[4,128,256]{2,1,0:T(8,128)S(1)} %get-tuple-element.31.a_ref), channel_id=1, source_target_pairs={{0,1},{1,0},{2,3},{3,2},{4,5},{5,4},{6,7},{7,6},{8,9},{9,8},{10,11... | collective-permute-start | bytes 1572872 | tf_op jit(solution)/shard_map/ppermute | solution.py:242
  45.3 11.8 %copy-start = (f32[1,1024,256]{2,1,0:T(8,128)S(1)}, f32[1,1024,256]{2,1,0:T(8,128)}, u32[]{:S(2)}) copy-start(f32[1,1024,256]{2,1,0:T(8,128)} %param.11) | copy-start | bytes 3145732
  45.3 24.1 %slice-start = ((s8[8388608]{0:T(1024)(128)(4,1)}), s8[4194304]{0:T(1024)(128)(4,1)S(1)}, s32[]{:S(2)}) async-start(s8[8388608]{0:T(1024)(128)(4,1)} %bitcast.13), calls=%async_computation.1 | async-start | bytes 8388608
  46.5 7.9 %collective-permute-start.15 = (f32[128,256]{1,0:T(8,128)S(1)}, f32[128,256]{1,0:T(8,128)S(1)}, u32[]{:S(2)}, u32[]{:S(2)}) collective-permute-start(f32[128,256]{1,0:T(8,128)S(1)} %get-tuple-element.42), channel_id=1, source_target_pairs={{0,16},{8,24},{16,0},{24,8},{1,17},{9,25},{17,1},{25,9},{2,18},{10... | collective-permute-start | bytes 393224 | tf_op jit(solution)/shard_map/ppermute | solution.py:235
  47.9 9.2 %collective-permute-start.16 = (f32[128,256]{1,0:T(8,128)S(1)}, f32[128,256]{1,0:T(8,128)S(1)}, u32[]{:S(2)}, u32[]{:S(2)}) collective-permute-start(f32[128,256]{1,0:T(8,128)S(1)} %get-tuple-element.43), channel_id=1, source_target_pairs={{0,8},{8,16},{16,24},{24,0},{1,9},{9,17},{17,25},{25,1},{2,10},{10... | collective-permute-start | bytes 393224 | tf_op jit(solution)/shard_map/ppermute | solution.py:235
  48.4 21.1 %slice-start.1 = ((s8[8388608]{0:T(1024)(128)(4,1)}), s8[4194304]{0:T(1024)(128)(4,1)S(1)}, s32[]{:S(2)}) async-start(s8[8388608]{0:T(1024)(128)(4,1)} %bitcast.13), calls=%async_computation.2 | async-start | bytes 8388608
  48.4 8.8 %collective-permute-start.17 = (f32[128,256]{1,0:T(8,128)S(1)}, f32[128,256]{1,0:T(8,128)S(1)}, u32[]{:S(2)}, u32[]{:S(2)}) collective-permute-start(f32[128,256]{1,0:T(8,128)S(1)} %get-tuple-element.44), channel_id=1, source_target_pairs={{0,24},{8,0},{16,8},{24,16},{1,25},{9,1},{17,9},{25,17},{2,26},{10... | collective-permute-start | bytes 393224 | tf_op jit(solution)/shard_map/ppermute | solution.py:235
  52.3 9.9 %collective-permute-start.4 = (f32[128,256]{1,0:T(8,128)S(1)}, f32[128,256]{1,0:T(8,128)S(1)}, u32[]{:S(2)}, u32[]{:S(2)}) collective-permute-start(f32[128,256]{1,0:T(8,128)S(1)} %get-tuple-element.34), channel_id=1, source_target_pairs={{0,16},{8,24},{16,0},{24,8},{1,17},{9,25},{17,1},{25,9},{2,18},{10... | collective-permute-start | bytes 393224 | tf_op jit(solution)/shard_map/ppermute | solution.py:235
  53.4 8.8 %collective-permute-start.5 = (f32[128,256]{1,0:T(8,128)S(1)}, f32[128,256]{1,0:T(8,128)S(1)}, u32[]{:S(2)}, u32[]{:S(2)}) collective-permute-start(f32[128,256]{1,0:T(8,128)S(1)} %get-tuple-element.35), channel_id=1, source_target_pairs={{0,8},{8,16},{16,24},{24,0},{1,9},{9,17},{17,25},{25,1},{2,10},{10... | collective-permute-start | bytes 393224 | tf_op jit(solution)/shard_map/ppermute | solution.py:235
  54.5 7.7 %collective-permute-start.6 = (f32[128,256]{1,0:T(8,128)S(1)}, f32[128,256]{1,0:T(8,128)S(1)}, u32[]{:S(2)}, u32[]{:S(2)}) collective-permute-start(f32[128,256]{1,0:T(8,128)S(1)} %get-tuple-element.36), channel_id=1, source_target_pairs={{0,24},{8,0},{16,8},{24,16},{1,25},{9,1},{17,9},{25,17},{2,26},{10... | collective-permute-start | bytes 393224 | tf_op jit(solution)/shard_map/ppermute | solution.py:235
  57.3 9.2 %collective-permute-start.20 = (f32[256,128]{1,0:T(8,128)S(1)}, f32[256,128]{1,0:T(8,128)S(1)}, u32[]{:S(2)}, u32[]{:S(2)}) collective-permute-start(f32[256,128]{1,0:T(8,128)S(1)} %reduce.3.a_ref), channel_id=1, source_target_pairs={{0,8},{8,16},{16,24},{24,0},{1,9},{9,17},{17,25},{25,1},{2,10},{10... | collective-permute-start | bytes 393224 | tf_op jit(solution)/shard_map/ppermute | solution.py:235
  59.4 10.0 %collective-permute-start.19 = (f32[256,128]{1,0:T(8,128)S(1)}, f32[256,128]{1,0:T(8,128)S(1)}, u32[]{:S(2)}, u32[]{:S(2)}) collective-permute-start(f32[256,128]{1,0:T(8,128)S(1)} %reduce.3.a_ref), channel_id=1, source_target_pairs={{0,16},{8,24},{16,0},{24,8},{1,17},{9,25},{17,1},{25,9},{2,18},{10... | collective-permute-start | bytes 393224 | tf_op jit(solution)/shard_map/ppermute | solution.py:235
  62.2 7.3 %collective-permute-start.18 = (f32[256,128]{1,0:T(8,128)S(1)}, f32[256,128]{1,0:T(8,128)S(1)}, u32[]{:S(2)}, u32[]{:S(2)}) collective-permute-start(f32[256,128]{1,0:T(8,128)S(1)} %reduce.3.a_ref), channel_id=1, source_target_pairs={{0,24},{8,0},{16,8},{24,16},{1,25},{9,1},{17,9},{25,17},{2,26},{10... | collective-permute-start | bytes 393224 | tf_op jit(solution)/shard_map/ppermute | solution.py:235
  62.3 9.6 %collective-permute-start.9 = (f32[256,128]{1,0:T(8,128)S(1)}, f32[256,128]{1,0:T(8,128)S(1)}, u32[]{:S(2)}, u32[]{:S(2)}) collective-permute-start(f32[256,128]{1,0:T(8,128)S(1)} %reduce.2.a_ref), channel_id=1, source_target_pairs={{0,8},{8,16},{16,24},{24,0},{1,9},{9,17},{17,25},{25,1},{2,10},{10... | collective-permute-start | bytes 393224 | tf_op jit(solution)/shard_map/ppermute | solution.py:235
  64.4 8.9 %collective-permute-start.8 = (f32[256,128]{1,0:T(8,128)S(1)}, f32[256,128]{1,0:T(8,128)S(1)}, u32[]{:S(2)}, u32[]{:S(2)}) collective-permute-start(f32[256,128]{1,0:T(8,128)S(1)} %reduce.2.a_ref), channel_id=1, source_target_pairs={{0,16},{8,24},{16,0},{24,8},{1,17},{9,25},{17,1},{25,9},{2,18},{10... | collective-permute-start | bytes 393224 | tf_op jit(solution)/shard_map/ppermute | solution.py:235
  66.5 6.9 %collective-permute-start.7 = (f32[256,128]{1,0:T(8,128)S(1)}, f32[256,128]{1,0:T(8,128)S(1)}, u32[]{:S(2)}, u32[]{:S(2)}) collective-permute-start(f32[256,128]{1,0:T(8,128)S(1)} %reduce.2.a_ref), channel_id=1, source_target_pairs={{0,24},{8,0},{16,8},{24,16},{1,25},{9,1},{17,9},{25,17},{2,26},{10... | collective-permute-start | bytes 393224 | tf_op jit(solution)/shard_map/ppermute | solution.py:235
  70.8 4.0 %collective-permute-start.21 = (f32[4,256,128]{2,1,0:T(8,128)S(1)}, f32[4,256,128]{2,1,0:T(8,128)S(1)}, u32[]{:S(2)}, u32[]{:S(2)}) collective-permute-start(f32[4,256,128]{2,1,0:T(8,128)S(1)} %send.3), channel_id=1, source_target_pairs={{0,1},{1,0},{2,3},{3,2},{4,5},{5,4},{6,7},{7,6},{8,9},{9,8},{10,11... | collective-permute-start | bytes 1572872 | tf_op jit(solution)/shard_map/ppermute | solution.py:242
  74.7 5.9 %collective-permute-start.10 = (f32[4,256,128]{2,1,0:T(8,128)S(1)}, f32[4,256,128]{2,1,0:T(8,128)S(1)}, u32[]{:S(2)}, u32[]{:S(2)}) collective-permute-start(f32[4,256,128]{2,1,0:T(8,128)S(1)} %send.2), channel_id=1, source_target_pairs={{0,1},{1,0},{2,3},{3,2},{4,5},{5,4},{6,7},{7,6},{8,9},{9,8},{10,11... | collective-permute-start | bytes 1572872 | tf_op jit(solution)/shard_map/ppermute | solution.py:242
  76.2 7.9 %collective-permute-start.22 = (f32[256,128]{1,0:T(8,128)S(1)}, f32[256,128]{1,0:T(8,128)S(1)}, u32[]{:S(2)}, u32[]{:S(2)}) collective-permute-start(f32[256,128]{1,0:T(8,128)S(1)} %get-tuple-element.46), channel_id=1, source_target_pairs={{0,4},{1,5},{2,6},{3,7},{4,0},{5,1},{6,2},{7,3},{8,12},{9,13},{10,... | collective-permute-start | bytes 393224 | tf_op jit(solution)/shard_map/ppermute | solution.py:238
  77.3 9.6 %collective-permute-start.23 = (f32[256,128]{1,0:T(8,128)S(1)}, f32[256,128]{1,0:T(8,128)S(1)}, u32[]{:S(2)}, u32[]{:S(2)}) collective-permute-start(f32[256,128]{1,0:T(8,128)S(1)} %get-tuple-element.47), channel_id=1, source_target_pairs={{0,2},{1,3},{2,4},{3,5},{4,6},{5,7},{6,0},{7,1},{8,10},{9,11},{10,... | collective-permute-start | bytes 393224 | tf_op jit(solution)/shard_map/ppermute | solution.py:238
  77.7 9.2 %collective-permute-start.24 = (f32[256,128]{1,0:T(8,128)S(1)}, f32[256,128]{1,0:T(8,128)S(1)}, u32[]{:S(2)}, u32[]{:S(2)}) collective-permute-start(f32[256,128]{1,0:T(8,128)S(1)} %get-tuple-element.48), channel_id=1, source_target_pairs={{0,6},{1,7},{2,0},{3,1},{4,2},{5,3},{6,4},{7,5},{8,14},{9,15},{10,... | collective-permute-start | bytes 393224 | tf_op jit(solution)/shard_map/ppermute | solution.py:238
  81.9 8.1 %collective-permute-start.11 = (f32[256,128]{1,0:T(8,128)S(1)}, f32[256,128]{1,0:T(8,128)S(1)}, u32[]{:S(2)}, u32[]{:S(2)}) collective-permute-start(f32[256,128]{1,0:T(8,128)S(1)} %get-tuple-element.38), channel_id=1, source_target_pairs={{0,4},{1,5},{2,6},{3,7},{4,0},{5,1},{6,2},{7,3},{8,12},{9,13},{10,... | collective-permute-start | bytes 393224 | tf_op jit(solution)/shard_map/ppermute | solution.py:238
  83.3 8.8 %collective-permute-start.12 = (f32[256,128]{1,0:T(8,128)S(1)}, f32[256,128]{1,0:T(8,128)S(1)}, u32[]{:S(2)}, u32[]{:S(2)}) collective-permute-start(f32[256,128]{1,0:T(8,128)S(1)} %get-tuple-element.39), channel_id=1, source_target_pairs={{0,2},{1,3},{2,4},{3,5},{4,6},{5,7},{6,0},{7,1},{8,10},{9,11},{10,... | collective-permute-start | bytes 393224 | tf_op jit(solution)/shard_map/ppermute | solution.py:238
  84.1 8.0 %collective-permute-start.13 = (f32[256,128]{1,0:T(8,128)S(1)}, f32[256,128]{1,0:T(8,128)S(1)}, u32[]{:S(2)}, u32[]{:S(2)}) collective-permute-start(f32[256,128]{1,0:T(8,128)S(1)} %get-tuple-element.40), channel_id=1, source_target_pairs={{0,6},{1,7},{2,0},{3,1},{4,2},{5,3},{6,4},{7,5},{8,14},{9,15},{10,... | collective-permute-start | bytes 393224 | tf_op jit(solution)/shard_map/ppermute | solution.py:238

commit v3 on v2

--- a/solution.py
+++ b/solution.py
@@ -112,7 +112,7 @@
         acc = [jnp.zeros((lanes, lanes), F32) for _ in range(2)]
         for p in range(SLOTS):
             rows = got_ref[pl.ds(2 * p + half, devices, stride=2 * SLOTS), :]
-            parts = split3(rows.T)
+            parts = split2(rows.T)
             for h in range(2):
                 choose = indicator(flag[h] & (count[h] == float(p + 1)))
                 for part in parts:
@@ -286,7 +286,7 @@
         name="load",
     )(placed, in_hbm(border_tile[0]))
     def send_z(own):
-        return {s: shift_z(own, s) for s in (2, 1, 3)}
+        return {s: shift_z(own, s) for s in (3, 1, 2)}
 
     def held(kernel, name, scratch, out_shape, *args):
         return pl.pallas_call(
@@ -319,12 +319,12 @@
                     [arr(width, quarter)] * n_row, in_vmem(tile), begun, other)
 
     def reduce(coupled, chunk):
-        arrived = [shift(coupled[(s + 2) % 4], s) for s in (2, 1, 3)]
+        arrived = [shift(coupled[(s + 2) % 4], s) for s in (3, 1, 2)]
         return held(functools.partial(reduce_kernel, chunk=chunk), "reduce", [],
                     arr(quarter, width), rhs, coupled[2], *arrived)
 
     def spread(reduced):
-        far, near, back = [shift(reduced, n_row - s) for s in (2, 1, 3)]
+        back, near, far = [shift(reduced, n_row - s) for s in (3, 1, 2)]
         return [reduced, near, far, back]
 
     def solve(pieces):
@@ -334,7 +334,7 @@
                     inverse, *pieces, swap(other))
 
     def finish(chip):
-        got = [shift_z(chip[(s + 2) % 4], s) for s in (2, 1, 3)]
+        got = [shift_z(chip[(s + 2) % 4], s) for s in (3, 1, 2)]
         return (chip[2] + got[0]) + (got[1] + got[2])
 
     chunks = range(CHUNKS)

time: 93.8 us -> 93.7 us (level)
  waiting for transfers between devices: 22.8 us -> 26.6 us
  starting transfers between devices: 28.4 us -> 25.4 us
    ppermute x12, waiting for transfers between devices: 6.79 us -> 10.2 us  [shift(): return lax.ppermute(x, 'row', [(i, (i + by) % n_row) for i in range(n_row)])]
    ppermute x12, starting transfers between devices: 17.1 us -> 14.6 us  [shift(): return lax.ppermute(x, 'row', [(i, (i + by) % n_row) for i in range(n_row)])]
  transfers between devices with their start and end apart: 25 -> 25, of which waited for: 13 -> 12; matrix products, arithmetic and copies ran while one was open for 0% -> 0% of each run, Pallas kernels for 11% -> 11%
where the time goes in v3:
time: 93.7 us; the launch traced here: 93.5 us
  waiting for transfers between devices  26.6 us (28%)
  starting transfers between devices  25.4 us (27%)
  blocking collectives  24.7 us (26%)
  Pallas kernels  15.9 us (17%)
    all_to_all x1, blocking collectives, shards(): lax.all_to_all(outgoing.reshape(devices, 2 * SLOTS, lanes), axes, split_a...  24.7 us
    ppermute x9, waiting for transfers between devices, shift_z(): lax.ppermute(x, 'col', [(2 * z + c, 2 * ((z + by) % n_z) + c) for z in ra...  16.4 us
    ppermute x12, starting transfers between devices, shift(): return lax.ppermute(x, 'row', [(i, (i + by) % n_row) for i in range(n_row)])  14.6 us
    ppermute x12, waiting for transfers between devices, shift(): return lax.ppermute(x, 'row', [(i, (i + by) % n_row) for i in range(n_row)])  10.2 us
    ppermute x9, starting transfers between devices, shift_z(): lax.ppermute(x, 'col', [(2 * z + c, 2 * ((z + by) % n_z) + c) for z in ra...  10.1 us
    pallas_call x9, Pallas kernels, held(): pl.pallas_call(kernel, in_specs=[vmem] * len(args), out_specs=jax.tree.ma...  9.77 us
    pallas_call x1, Pallas kernels, shards(): pl.pallas_call(load_kernel, in_specs=[anywhere, hbm], out_specs=[vmem, vm...  3.5 us
  transfers between devices with their start and end apart: 25, of which 12 were waited for; matrix products, arithmetic and copies ran while one was open for 0% of the time, Pallas kernels for 11%

profile of v3, /device:TPU:0, one launch (start us, length us, event | category | flops | bytes accessed | tf_op | source)
XLA Modules:
  0.0 93.5 jit_solution(18098926903122153058)
XLA Ops:
  0.0 1.8 %pick.1 = (f32[1024,128]{1,0:T(8,128)S(1)}, s32[2,128]{1,0:T(2,128)S(1)}) custom-call(s32[256,128]{1,0:T(8,128)} %bitcast.24, s32[256,128]{1,0:T(8,128)} %bitcast.25, f32[128,256]{1,0:T(8,128)} %parent_hbm.1), custom_call_target="tpu_custom_call" | custom-call | tf_op jit(solution)/shard_map/pick/pallas_call | solution.py:255
  1.9 24.7 %all_to_all.5 = f32[128,8,128]{2,1,0:T(8,128)S(1)} all-to-all(f32[128,8,128]{2,1,0:T(8,128)S(1)} %bitcast.22), channel_id=1, replica_groups=mesh['child'=4,'row'=4,'col'=8] {'child','row','col'}, dimensions={0} | all-to-all | bytes 1048576 | tf_op jit(solution)/shard_map/all_to_all | solution.py:265
  26.5 0.7 place.1.order_ref.a_ref
  27.2 0.2 collective-permute-start.2
  27.4 2.1 %collective-permute-start.1 = (f32[256,256]{1,0:T(8,128)S(1)}, f32[256,256]{1,0:T(8,128)S(1)}, u32[]{:S(2)}, u32[]{:S(2)}) collective-permute-start(f32[256,256]{1,0:T(8,128)S(1)} %place.1.order_ref.a_ref), channel_id=1, source_target_pairs={{0,4},{1,5},{2,6},{3,7},{4,0},{5,1},{6,2},{7,3},{8,12},{9,13},{10,... | collective-permute-start | bytes 786440 | tf_op jit(solution)/shard_map/ppermute | solution.py:238
  29.6 3.5 %load.1 = (f32[2048,1024]{1,0:T(8,128)S(1)}, f32[8,128]{1,0:T(8,128)S(1)}) custom-call(f32[256,256]{1,0:T(8,128)S(1)} %place.1.order_ref.a_ref, f32[2048,1024]{1,0:T(8,128)} %bitcast.23), custom_call_target="tpu_custom_call" | custom-call | bytes 16777216 | tf_op jit(solution)/shard_map/load/pallas_call | solution.py:277
  33.1 3.4 %collective-permute-done.2.d_ref = f32[256,256]{1,0:T(8,128)S(1)} collective-permute-done((f32[256,256]{1,0:T(8,128)S(1)}, f32[256,256]{1,0:T(8,128)S(1)}, u32[]{:S(2)}, u32[]{:S(2)}) %collective-permute-start.2) | collective-permute-done | bytes 262176 | tf_op jit(solution)/shard_map/ppermute | solution.py:238
  36.5 1.6 %collective-permute-done.1.c_ref = f32[256,256]{1,0:T(8,128)S(1)} collective-permute-done((f32[256,256]{1,0:T(8,128)S(1)}, f32[256,256]{1,0:T(8,128)S(1)}, u32[]{:S(2)}, u32[]{:S(2)}) %collective-permute-start.1) | collective-permute-done | bytes 262176 | tf_op jit(solution)/shard_map/ppermute | solution.py:238
  38.1 4.6 %collective-permute-done.b_ref = f32[256,256]{1,0:T(8,128)S(1)} collective-permute-done((f32[256,256]{1,0:T(8,128)S(1)}, f32[256,256]{1,0:T(8,128)S(1)}, u32[]{:S(2)}, u32[]{:S(2)}) %collective-permute-start) | collective-permute-done | bytes 262176 | tf_op jit(solution)/shard_map/ppermute | solution.py:238
  42.8 0.1 collective-permute-start.14
  42.9 0.5 collective-permute-start.3
  43.4 1.8 %begin.1.sum_ref = f32[4,256,256]{2,1,0:T(8,128)S(1)} custom-call(f32[2048,1024]{1,0:T(8,128)S(1)} %get-tuple-element.29.tile_ref, f32[4,128,256]{2,1,0:T(8,128)S(1)} %get-tuple-element.31.a_ref, f32[4,128,256]{2,1,0:T(8,128)S(1)} %get-tuple-element.32.b_ref), custom_call_target="tpu_custom_call" | custom-call | tf_op jit(solution)/shard_map/begin/pallas_call | solution.py:292
  45.2 1.2 %couple.3 = (f32[128,256]{1,0:T(8,128)S(1)}, f32[128,256]{1,0:T(8,128)S(1)}, f32[128,256]{1,0:T(8,128)S(1)}, f32[128,256]{1,0:T(8,128)S(1)}) custom-call(f32[2048,1024]{1,0:T(8,128)S(1)} %get-tuple-element.29.tile_ref, f32[4,256,256]{2,1,0:T(8,128)S(1)} %begin.1.sum_ref, f32[4,128,256]{2,1,0:T(8,128)S(1)} %collective-permute-done.14.other_ref), custom_call_target="tpu_custom_call" | custom-call | tf_op jit(solution)/shard_map/couple/pallas_call | solution.py:292
  46.4 0.9 %collective-permute-start.15 = (f32[128,256]{1,0:T(8,128)S(1)}, f32[128,256]{1,0:T(8,128)S(1)}, u32[]{:S(2)}, u32[]{:S(2)}) collective-permute-start(f32[128,256]{1,0:T(8,128)S(1)} %get-tuple-element.42), channel_id=1, source_target_pairs={{0,24},{8,0},{16,8},{24,16},{1,25},{9,1},{17,9},{25,17},{2,26},{10... | collective-permute-start | bytes 393224 | tf_op jit(solution)/shard_map/ppermute | solution.py:235
  47.3 1.1 %collective-permute-start.16 = (f32[128,256]{1,0:T(8,128)S(1)}, f32[128,256]{1,0:T(8,128)S(1)}, u32[]{:S(2)}, u32[]{:S(2)}) collective-permute-start(f32[128,256]{1,0:T(8,128)S(1)} %get-tuple-element.43), channel_id=1, source_target_pairs={{0,8},{8,16},{16,24},{24,0},{1,9},{9,17},{17,25},{25,1},{2,10},{10... | collective-permute-start | bytes 393224 | tf_op jit(solution)/shard_map/ppermute | solution.py:235
  48.5 1.3 %collective-permute-start.17 = (f32[128,256]{1,0:T(8,128)S(1)}, f32[128,256]{1,0:T(8,128)S(1)}, u32[]{:S(2)}, u32[]{:S(2)}) collective-permute-start(f32[128,256]{1,0:T(8,128)S(1)} %get-tuple-element.44), channel_id=1, source_target_pairs={{0,16},{8,24},{16,0},{24,8},{1,17},{9,25},{17,1},{25,9},{2,18},{10... | collective-permute-start | bytes 393224 | tf_op jit(solution)/shard_map/ppermute | solution.py:235
  49.8 1.2 %couple.2 = (f32[128,256]{1,0:T(8,128)S(1)}, f32[128,256]{1,0:T(8,128)S(1)}, f32[128,256]{1,0:T(8,128)S(1)}, f32[128,256]{1,0:T(8,128)S(1)}) custom-call(f32[2048,1024]{1,0:T(8,128)S(1)} %get-tuple-element.29.tile_ref, f32[4,256,256]{2,1,0:T(8,128)S(1)} %begin.1.sum_ref, f32[4,128,256]{2,1,0:T(8,128)S(1)} %collective-permute-done.3.other_ref), custom_call_target="tpu_custom_call" | custom-call | tf_op jit(solution)/shard_map/couple/pallas_call | solution.py:292
  50.9 2.0 %collective-permute-start.4 = (f32[128,256]{1,0:T(8,128)S(1)}, f32[128,256]{1,0:T(8,128)S(1)}, u32[]{:S(2)}, u32[]{:S(2)}) collective-permute-start(f32[128,256]{1,0:T(8,128)S(1)} %get-tuple-element.34), channel_id=1, source_target_pairs={{0,24},{8,0},{16,8},{24,16},{1,25},{9,1},{17,9},{25,17},{2,26},{10... | collective-permute-start | bytes 393224 | tf_op jit(solution)/shard_map/ppermute | solution.py:235
  52.9 0.1 collective-permute-start.5
  53.0 2.2 %collective-permute-start.6 = (f32[128,256]{1,0:T(8,128)S(1)}, f32[128,256]{1,0:T(8,128)S(1)}, u32[]{:S(2)}, u32[]{:S(2)}) collective-permute-start(f32[128,256]{1,0:T(8,128)S(1)} %get-tuple-element.36), channel_id=1, source_target_pairs={{0,16},{8,24},{16,0},{24,8},{1,17},{9,25},{17,1},{25,9},{2,18},{10... | collective-permute-start | bytes 393224 | tf_op jit(solution)/shard_map/ppermute | solution.py:235
  55.3 1.6 %collective-permute-done.16.c_ref = f32[128,256]{1,0:T(8,128)S(1)} collective-permute-done((f32[128,256]{1,0:T(8,128)S(1)}, f32[128,256]{1,0:T(8,128)S(1)}, u32[]{:S(2)}, u32[]{:S(2)}) %collective-permute-start.16) | collective-permute-done | bytes 131104 | tf_op jit(solution)/shard_map/ppermute | solution.py:235
  56.9 0.1 reduce.3.a_ref
  57.0 0.2 collective-permute-start.20
  57.2 2.9 %collective-permute-start.19 = (f32[256,128]{1,0:T(8,128)S(1)}, f32[256,128]{1,0:T(8,128)S(1)}, u32[]{:S(2)}, u32[]{:S(2)}) collective-permute-start(f32[256,128]{1,0:T(8,128)S(1)} %reduce.3.a_ref), channel_id=1, source_target_pairs={{0,16},{8,24},{16,0},{24,8},{1,17},{9,25},{17,1},{25,9},{2,18},{10... | collective-permute-start | bytes 393224 | tf_op jit(solution)/shard_map/ppermute | solution.py:235
  60.2 1.8 %collective-permute-start.18 = (f32[256,128]{1,0:T(8,128)S(1)}, f32[256,128]{1,0:T(8,128)S(1)}, u32[]{:S(2)}, u32[]{:S(2)}) collective-permute-start(f32[256,128]{1,0:T(8,128)S(1)} %reduce.3.a_ref), channel_id=1, source_target_pairs={{0,24},{8,0},{16,8},{24,16},{1,25},{9,1},{17,9},{25,17},{2,26},{10... | collective-permute-start | bytes 393224 | tf_op jit(solution)/shard_map/ppermute | solution.py:235
  62.0 1.4 %collective-permute-done.5.c_ref = f32[128,256]{1,0:T(8,128)S(1)} collective-permute-done((f32[128,256]{1,0:T(8,128)S(1)}, f32[128,256]{1,0:T(8,128)S(1)}, u32[]{:S(2)}, u32[]{:S(2)}) %collective-permute-start.5) | collective-permute-done | bytes 131104 | tf_op jit(solution)/shard_map/ppermute | solution.py:235
  63.4 0.1 reduce.2.a_ref
  63.6 1.8 %collective-permute-start.8 = (f32[256,128]{1,0:T(8,128)S(1)}, f32[256,128]{1,0:T(8,128)S(1)}, u32[]{:S(2)}, u32[]{:S(2)}) collective-permute-start(f32[256,128]{1,0:T(8,128)S(1)} %reduce.2.a_ref), channel_id=1, source_target_pairs={{0,16},{8,24},{16,0},{24,8},{1,17},{9,25},{17,1},{25,9},{2,18},{10... | collective-permute-start | bytes 393224 | tf_op jit(solution)/shard_map/ppermute | solution.py:235
  65.4 3.6 %collective-permute-done.20.d_ref = f32[256,128]{1,0:T(8,128)S(1)} collective-permute-done((f32[256,128]{1,0:T(8,128)S(1)}, f32[256,128]{1,0:T(8,128)S(1)}, u32[]{:S(2)}, u32[]{:S(2)}) %collective-permute-start.20) | collective-permute-done | bytes 131104 | tf_op jit(solution)/shard_map/ppermute | solution.py:235
  69.1 1.4 %send.3 = f32[4,256,128]{2,1,0:T(8,128)S(1)} custom-call(f32[2048,1024]{1,0:T(8,128)S(1)} %bitcast.15, f32[256,128]{1,0:T(8,128)S(1)} %reduce.3.a_ref, f32[256,128]{1,0:T(8,128)S(1)} %collective-permute-done.18.b_ref, f32[256,128]{1,0:T(8,128)S(1)} %collective-permute-done.19.c_ref, f32[256,128]{1,0:T(8,128)S(1)} %collective-permute-done.20.d_ref), custom_call_target="tpu_custom_call" | custom-call | tf_op jit(solution)/shard_map/send/pallas_call | solution.py:292
  70.5 0.1 collective-permute-start.21
  70.6 2.9 %collective-permute-done.9.d_ref = f32[256,128]{1,0:T(8,128)S(1)} collective-permute-done((f32[256,128]{1,0:T(8,128)S(1)}, f32[256,128]{1,0:T(8,128)S(1)}, u32[]{:S(2)}, u32[]{:S(2)}) %collective-permute-start.9) | collective-permute-done | bytes 131104 | tf_op jit(solution)/shard_map/ppermute | solution.py:235
  73.4 0.6 collective-permute-done.7.b_ref
  74.0 1.4 %send.2 = f32[4,256,128]{2,1,0:T(8,128)S(1)} custom-call(f32[2048,1024]{1,0:T(8,128)S(1)} %bitcast.16, f32[256,128]{1,0:T(8,128)S(1)} %reduce.2.a_ref, f32[256,128]{1,0:T(8,128)S(1)} %collective-permute-done.7.b_ref, f32[256,128]{1,0:T(8,128)S(1)} %collective-permute-done.8.c_ref, f32[256,128]{1,0:T(8,128)S(1)} %collective-permute-done.9.d_ref), custom_call_target="tpu_custom_call" | custom-call | tf_op jit(solution)/shard_map/send/pallas_call | solution.py:292
  75.4 0.1 collective-permute-start.10
  75.5 1.4 %keep.3 = (f32[256,128]{1,0:T(8,128)S(1)}, f32[256,128]{1,0:T(8,128)S(1)}, f32[256,128]{1,0:T(8,128)S(1)}, f32[256,128]{1,0:T(8,128)S(1)}) custom-call(f32[2048,1024]{1,0:T(8,128)S(1)} %bitcast.17, f32[256,128]{1,0:T(8,128)S(1)} %reduce.3.a_ref, f32[256,128]{1,0:T(8,128)S(1)} %collective-permute-done.18.b_ref, f32[256,128]{1,0:T(8,128)S(1)} %collective-permute-done.19.c_ref, ...), custom_call_target="tpu_custom_call" | custom-call | tf_op jit(solution)/shard_map/keep/pallas_call | solution.py:292
  76.9 0.7 collective-permute-start.22
  77.5 1.4 %collective-permute-start.23 = (f32[256,128]{1,0:T(8,128)S(1)}, f32[256,128]{1,0:T(8,128)S(1)}, u32[]{:S(2)}, u32[]{:S(2)}) collective-permute-start(f32[256,128]{1,0:T(8,128)S(1)} %get-tuple-element.47), channel_id=1, source_target_pairs={{0,2},{1,3},{2,4},{3,5},{4,6},{5,7},{6,0},{7,1},{8,10},{9,11},{10,... | collective-permute-start | bytes 393224 | tf_op jit(solution)/shard_map/ppermute | solution.py:238
  79.0 1.3 %collective-permute-start.24 = (f32[256,128]{1,0:T(8,128)S(1)}, f32[256,128]{1,0:T(8,128)S(1)}, u32[]{:S(2)}, u32[]{:S(2)}) collective-permute-start(f32[256,128]{1,0:T(8,128)S(1)} %get-tuple-element.48), channel_id=1, source_target_pairs={{0,4},{1,5},{2,6},{3,7},{4,0},{5,1},{6,2},{7,3},{8,12},{9,13},{10,... | collective-permute-start | bytes 393224 | tf_op jit(solution)/shard_map/ppermute | solution.py:238
  80.3 1.4 %keep.2 = (f32[256,128]{1,0:T(8,128)S(1)}, f32[256,128]{1,0:T(8,128)S(1)}, f32[256,128]{1,0:T(8,128)S(1)}, f32[256,128]{1,0:T(8,128)S(1)}) custom-call(f32[2048,1024]{1,0:T(8,128)S(1)} %bitcast.18, f32[256,128]{1,0:T(8,128)S(1)} %reduce.2.a_ref, f32[256,128]{1,0:T(8,128)S(1)} %collective-permute-done.7.b_ref, f32[256,128]{1,0:T(8,128)S(1)} %collective-permute-done.8.c_ref, ...), custom_call_target="tpu_custom_call" | custom-call | tf_op jit(solution)/shard_map/keep/pallas_call | solution.py:292
  81.6 1.4 %collective-permute-start.11 = (f32[256,128]{1,0:T(8,128)S(1)}, f32[256,128]{1,0:T(8,128)S(1)}, u32[]{:S(2)}, u32[]{:S(2)}) collective-permute-start(f32[256,128]{1,0:T(8,128)S(1)} %get-tuple-element.38), channel_id=1, source_target_pairs={{0,6},{1,7},{2,0},{3,1},{4,2},{5,3},{6,4},{7,5},{8,14},{9,15},{10,... | collective-permute-start | bytes 393224 | tf_op jit(solution)/shard_map/ppermute | solution.py:238
  83.1 0.7 collective-permute-start.12
  83.7 2.2 %collective-permute-start.13 = (f32[256,128]{1,0:T(8,128)S(1)}, f32[256,128]{1,0:T(8,128)S(1)}, u32[]{:S(2)}, u32[]{:S(2)}) collective-permute-start(f32[256,128]{1,0:T(8,128)S(1)} %get-tuple-element.40), channel_id=1, source_target_pairs={{0,4},{1,5},{2,6},{3,7},{4,0},{5,1},{6,2},{7,3},{8,12},{9,13},{10,... | collective-permute-start | bytes 393224 | tf_op jit(solution)/shard_map/ppermute | solution.py:238
  86.0 1.1 %collective-permute-done.23 = f32[256,128]{1,0:T(8,128)S(1)} collective-permute-done((f32[256,128]{1,0:T(8,128)S(1)}, f32[256,128]{1,0:T(8,128)S(1)}, u32[]{:S(2)}, u32[]{:S(2)}) %collective-permute-start.23) | collective-permute-done | bytes 131104 | tf_op jit(solution)/shard_map/ppermute | solution.py:238
  87.1 0.3 collective-permute-done.24
  87.5 1.4 %collective-permute-done.11 = f32[256,128]{1,0:T(8,128)S(1)} collective-permute-done((f32[256,128]{1,0:T(8,128)S(1)}, f32[256,128]{1,0:T(8,128)S(1)}, u32[]{:S(2)}, u32[]{:S(2)}) %collective-permute-start.11) | collective-permute-done | bytes 131104 | tf_op jit(solution)/shard_map/ppermute | solution.py:238
  88.8 3.9 %collective-permute-done.12 = f32[256,128]{1,0:T(8,128)S(1)} collective-permute-done((f32[256,128]{1,0:T(8,128)S(1)}, f32[256,128]{1,0:T(8,128)S(1)}, u32[]{:S(2)}, u32[]{:S(2)}) %collective-permute-start.12) | collective-permute-done | bytes 131104 | tf_op jit(solution)/shard_map/ppermute | solution.py:238
  92.8 0.7 maximum_bitcast_fusion
  (26 shorter events, 0.3 us)
Async XLA Ops:
  27.2 9.3 %collective-permute-start.2 = (f32[256,256]{1,0:T(8,128)S(1)}, f32[256,256]{1,0:T(8,128)S(1)}, u32[]{:S(2)}, u32[]{:S(2)}) collective-permute-start(f32[256,256]{1,0:T(8,128)S(1)} %place.1.order_ref.a_ref), channel_id=1, source_target_pairs={{0,6},{1,7},{2,0},{3,1},{4,2},{5,3},{6,4},{7,5},{8,14},{9,15},{10,... | collective-permute-start | bytes 786440 | tf_op jit(solution)/shard_map/ppermute | solution.py:238
  27.4 10.7 %collective-permute-start.1 = (f32[256,256]{1,0:T(8,128)S(1)}, f32[256,256]{1,0:T(8,128)S(1)}, u32[]{:S(2)}, u32[]{:S(2)}) collective-permute-start(f32[256,256]{1,0:T(8,128)S(1)} %place.1.order_ref.a_ref), channel_id=1, source_target_pairs={{0,4},{1,5},{2,6},{3,7},{4,0},{5,1},{6,2},{7,3},{8,12},{9,13},{10,... | collective-permute-start | bytes 786440 | tf_op jit(solution)/shard_map/ppermute | solution.py:238
  29.5 13.2 %collective-permute-start = (f32[256,256]{1,0:T(8,128)S(1)}, f32[256,256]{1,0:T(8,128)S(1)}, u32[]{:S(2)}, u32[]{:S(2)}) collective-permute-start(f32[256,256]{1,0:T(8,128)S(1)} %place.1.order_ref.a_ref), channel_id=1, source_target_pairs={{0,2},{1,3},{2,4},{3,5},{4,6},{5,7},{6,0},{7,1},{8,10},{9,11},{10,... | collective-permute-start | bytes 786440 | tf_op jit(solution)/shard_map/ppermute | solution.py:238
  42.8 2.4 %collective-permute-start.14 = (f32[4,128,256]{2,1,0:T(8,128)S(1)}, f32[4,128,256]{2,1,0:T(8,128)S(1)}, u32[]{:S(2)}, u32[]{:S(2)}) collective-permute-start(f32[4,128,256]{2,1,0:T(8,128)S(1)} %get-tuple-element.32.b_ref), channel_id=1, source_target_pairs={{0,1},{1,0},{2,3},{3,2},{4,5},{5,4},{6,7},{7,6},{8,9},{9,8},{10,11... | collective-permute-start | bytes 1572872 | tf_op jit(solution)/shard_map/ppermute | solution.py:242
  42.9 6.9 %collective-permute-start.3 = (f32[4,128,256]{2,1,0:T(8,128)S(1)}, f32[4,128,256]{2,1,0:T(8,128)S(1)}, u32[]{:S(2)}, u32[]{:S(2)}) collective-permute-start(f32[4,128,256]{2,1,0:T(8,128)S(1)} %get-tuple-element.31.a_ref), channel_id=1, source_target_pairs={{0,1},{1,0},{2,3},{3,2},{4,5},{5,4},{6,7},{7,6},{8,9},{9,8},{10,11... | collective-permute-start | bytes 1572872 | tf_op jit(solution)/shard_map/ppermute | solution.py:242
  45.2 11.7 %copy-start = (f32[1,1024,256]{2,1,0:T(8,128)S(1)}, f32[1,1024,256]{2,1,0:T(8,128)}, u32[]{:S(2)}) copy-start(f32[1,1024,256]{2,1,0:T(8,128)} %param.11) | copy-start | bytes 3145732
  45.2 23.9 %slice-start = ((s8[8388608]{0:T(1024)(128)(4,1)}), s8[4194304]{0:T(1024)(128)(4,1)S(1)}, s32[]{:S(2)}) async-start(s8[8388608]{0:T(1024)(128)(4,1)} %bitcast.13), calls=%async_computation.1 | async-start | bytes 8388608
  46.4 6.7 %collective-permute-start.15 = (f32[128,256]{1,0:T(8,128)S(1)}, f32[128,256]{1,0:T(8,128)S(1)}, u32[]{:S(2)}, u32[]{:S(2)}) collective-permute-start(f32[128,256]{1,0:T(8,128)S(1)} %get-tuple-element.42), channel_id=1, source_target_pairs={{0,24},{8,0},{16,8},{24,16},{1,25},{9,1},{17,9},{25,17},{2,26},{10... | collective-permute-start | bytes 393224 | tf_op jit(solution)/shard_map/ppermute | solution.py:235
  47.3 9.6 %collective-permute-start.16 = (f32[128,256]{1,0:T(8,128)S(1)}, f32[128,256]{1,0:T(8,128)S(1)}, u32[]{:S(2)}, u32[]{:S(2)}) collective-permute-start(f32[128,256]{1,0:T(8,128)S(1)} %get-tuple-element.43), channel_id=1, source_target_pairs={{0,8},{8,16},{16,24},{24,0},{1,9},{9,17},{17,25},{25,1},{2,10},{10... | collective-permute-start | bytes 393224 | tf_op jit(solution)/shard_map/ppermute | solution.py:235
  48.5 20.6 %slice-start.1 = ((s8[8388608]{0:T(1024)(128)(4,1)}), s8[4194304]{0:T(1024)(128)(4,1)S(1)}, s32[]{:S(2)}) async-start(s8[8388608]{0:T(1024)(128)(4,1)} %bitcast.13), calls=%async_computation.2 | async-start | bytes 8388608
  48.5 8.4 %collective-permute-start.17 = (f32[128,256]{1,0:T(8,128)S(1)}, f32[128,256]{1,0:T(8,128)S(1)}, u32[]{:S(2)}, u32[]{:S(2)}) collective-permute-start(f32[128,256]{1,0:T(8,128)S(1)} %get-tuple-element.44), channel_id=1, source_target_pairs={{0,16},{8,24},{16,0},{24,8},{1,17},{9,25},{17,1},{25,9},{2,18},{10... | collective-permute-start | bytes 393224 | tf_op jit(solution)/shard_map/ppermute | solution.py:235
  50.9 9.2 %collective-permute-start.4 = (f32[128,256]{1,0:T(8,128)S(1)}, f32[128,256]{1,0:T(8,128)S(1)}, u32[]{:S(2)}, u32[]{:S(2)}) collective-permute-start(f32[128,256]{1,0:T(8,128)S(1)} %get-tuple-element.34), channel_id=1, source_target_pairs={{0,24},{8,0},{16,8},{24,16},{1,25},{9,1},{17,9},{25,17},{2,26},{10... | collective-permute-start | bytes 393224 | tf_op jit(solution)/shard_map/ppermute | solution.py:235
  52.9 10.5 %collective-permute-start.5 = (f32[128,256]{1,0:T(8,128)S(1)}, f32[128,256]{1,0:T(8,128)S(1)}, u32[]{:S(2)}, u32[]{:S(2)}) collective-permute-start(f32[128,256]{1,0:T(8,128)S(1)} %get-tuple-element.35), channel_id=1, source_target_pairs={{0,8},{8,16},{16,24},{24,0},{1,9},{9,17},{17,25},{25,1},{2,10},{10... | collective-permute-start | bytes 393224 | tf_op jit(solution)/shard_map/ppermute | solution.py:235
  53.0 10.4 %collective-permute-start.6 = (f32[128,256]{1,0:T(8,128)S(1)}, f32[128,256]{1,0:T(8,128)S(1)}, u32[]{:S(2)}, u32[]{:S(2)}) collective-permute-start(f32[128,256]{1,0:T(8,128)S(1)} %get-tuple-element.36), channel_id=1, source_target_pairs={{0,16},{8,24},{16,0},{24,8},{1,17},{9,25},{17,1},{25,9},{2,18},{10... | collective-permute-start | bytes 393224 | tf_op jit(solution)/shard_map/ppermute | solution.py:235
  57.0 12.0 %collective-permute-start.20 = (f32[256,128]{1,0:T(8,128)S(1)}, f32[256,128]{1,0:T(8,128)S(1)}, u32[]{:S(2)}, u32[]{:S(2)}) collective-permute-start(f32[256,128]{1,0:T(8,128)S(1)} %reduce.3.a_ref), channel_id=1, source_target_pairs={{0,8},{8,16},{16,24},{24,0},{1,9},{9,17},{17,25},{25,1},{2,10},{10... | collective-permute-start | bytes 393224 | tf_op jit(solution)/shard_map/ppermute | solution.py:235
  57.2 11.9 %collective-permute-start.19 = (f32[256,128]{1,0:T(8,128)S(1)}, f32[256,128]{1,0:T(8,128)S(1)}, u32[]{:S(2)}, u32[]{:S(2)}) collective-permute-start(f32[256,128]{1,0:T(8,128)S(1)} %reduce.3.a_ref), channel_id=1, source_target_pairs={{0,16},{8,24},{16,0},{24,8},{1,17},{9,25},{17,1},{25,9},{2,18},{10... | collective-permute-start | bytes 393224 | tf_op jit(solution)/shard_map/ppermute | solution.py:235
  60.2 8.9 %collective-permute-start.18 = (f32[256,128]{1,0:T(8,128)S(1)}, f32[256,128]{1,0:T(8,128)S(1)}, u32[]{:S(2)}, u32[]{:S(2)}) collective-permute-start(f32[256,128]{1,0:T(8,128)S(1)} %reduce.3.a_ref), channel_id=1, source_target_pairs={{0,24},{8,0},{16,8},{24,16},{1,25},{9,1},{17,9},{25,17},{2,26},{10... | collective-permute-start | bytes 393224 | tf_op jit(solution)/shard_map/ppermute | solution.py:235
  63.5 9.9 %collective-permute-start.9 = (f32[256,128]{1,0:T(8,128)S(1)}, f32[256,128]{1,0:T(8,128)S(1)}, u32[]{:S(2)}, u32[]{:S(2)}) collective-permute-start(f32[256,128]{1,0:T(8,128)S(1)} %reduce.2.a_ref), channel_id=1, source_target_pairs={{0,8},{8,16},{16,24},{24,0},{1,9},{9,17},{17,25},{25,1},{2,10},{10... | collective-permute-start | bytes 393224 | tf_op jit(solution)/shard_map/ppermute | solution.py:235
  63.6 9.8 %collective-permute-start.8 = (f32[256,128]{1,0:T(8,128)S(1)}, f32[256,128]{1,0:T(8,128)S(1)}, u32[]{:S(2)}, u32[]{:S(2)}) collective-permute-start(f32[256,128]{1,0:T(8,128)S(1)} %reduce.2.a_ref), channel_id=1, source_target_pairs={{0,16},{8,24},{16,0},{24,8},{1,17},{9,25},{17,1},{25,9},{2,18},{10... | collective-permute-start | bytes 393224 | tf_op jit(solution)/shard_map/ppermute | solution.py:235
  69.1 5.0 %collective-permute-start.7 = (f32[256,128]{1,0:T(8,128)S(1)}, f32[256,128]{1,0:T(8,128)S(1)}, u32[]{:S(2)}, u32[]{:S(2)}) collective-permute-start(f32[256,128]{1,0:T(8,128)S(1)} %reduce.2.a_ref), channel_id=1, source_target_pairs={{0,24},{8,0},{16,8},{24,16},{1,25},{9,1},{17,9},{25,17},{2,26},{10... | collective-permute-start | bytes 393224 | tf_op jit(solution)/shard_map/ppermute | solution.py:235
  70.5 5.0 %collective-permute-start.21 = (f32[4,256,128]{2,1,0:T(8,128)S(1)}, f32[4,256,128]{2,1,0:T(8,128)S(1)}, u32[]{:S(2)}, u32[]{:S(2)}) collective-permute-start(f32[4,256,128]{2,1,0:T(8,128)S(1)} %send.3), channel_id=1, source_target_pairs={{0,1},{1,0},{2,3},{3,2},{4,5},{5,4},{6,7},{7,6},{8,9},{9,8},{10,11... | collective-permute-start | bytes 1572872 | tf_op jit(solution)/shard_map/ppermute | solution.py:242
  75.4 4.9 %collective-permute-start.10 = (f32[4,256,128]{2,1,0:T(8,128)S(1)}, f32[4,256,128]{2,1,0:T(8,128)S(1)}, u32[]{:S(2)}, u32[]{:S(2)}) collective-permute-start(f32[4,256,128]{2,1,0:T(8,128)S(1)} %send.2), channel_id=1, source_target_pairs={{0,1},{1,0},{2,3},{3,2},{4,5},{5,4},{6,7},{7,6},{8,9},{9,8},{10,11... | collective-permute-start | bytes 1572872 | tf_op jit(solution)/shard_map/ppermute | solution.py:242
  76.9 6.9 %collective-permute-start.22 = (f32[256,128]{1,0:T(8,128)S(1)}, f32[256,128]{1,0:T(8,128)S(1)}, u32[]{:S(2)}, u32[]{:S(2)}) collective-permute-start(f32[256,128]{1,0:T(8,128)S(1)} %get-tuple-element.46), channel_id=1, source_target_pairs={{0,6},{1,7},{2,0},{3,1},{4,2},{5,3},{6,4},{7,5},{8,14},{9,15},{10,... | collective-permute-start | bytes 393224 | tf_op jit(solution)/shard_map/ppermute | solution.py:238
  77.5 9.6 %collective-permute-start.23 = (f32[256,128]{1,0:T(8,128)S(1)}, f32[256,128]{1,0:T(8,128)S(1)}, u32[]{:S(2)}, u32[]{:S(2)}) collective-permute-start(f32[256,128]{1,0:T(8,128)S(1)} %get-tuple-element.47), channel_id=1, source_target_pairs={{0,2},{1,3},{2,4},{3,5},{4,6},{5,7},{6,0},{7,1},{8,10},{9,11},{10,... | collective-permute-start | bytes 393224 | tf_op jit(solution)/shard_map/ppermute | solution.py:238
  79.0 8.5 %collective-permute-start.24 = (f32[256,128]{1,0:T(8,128)S(1)}, f32[256,128]{1,0:T(8,128)S(1)}, u32[]{:S(2)}, u32[]{:S(2)}) collective-permute-start(f32[256,128]{1,0:T(8,128)S(1)} %get-tuple-element.48), channel_id=1, source_target_pairs={{0,4},{1,5},{2,6},{3,7},{4,0},{5,1},{6,2},{7,3},{8,12},{9,13},{10,... | collective-permute-start | bytes 393224 | tf_op jit(solution)/shard_map/ppermute | solution.py:238
  81.6 7.2 %collective-permute-start.11 = (f32[256,128]{1,0:T(8,128)S(1)}, f32[256,128]{1,0:T(8,128)S(1)}, u32[]{:S(2)}, u32[]{:S(2)}) collective-permute-start(f32[256,128]{1,0:T(8,128)S(1)} %get-tuple-element.38), channel_id=1, source_target_pairs={{0,6},{1,7},{2,0},{3,1},{4,2},{5,3},{6,4},{7,5},{8,14},{9,15},{10,... | collective-permute-start | bytes 393224 | tf_op jit(solution)/shard_map/ppermute | solution.py:238
  83.1 9.7 %collective-permute-start.12 = (f32[256,128]{1,0:T(8,128)S(1)}, f32[256,128]{1,0:T(8,128)S(1)}, u32[]{:S(2)}, u32[]{:S(2)}) collective-permute-start(f32[256,128]{1,0:T(8,128)S(1)} %get-tuple-element.39), channel_id=1, source_target_pairs={{0,2},{1,3},{2,4},{3,5},{4,6},{5,7},{6,0},{7,1},{8,10},{9,11},{10,... | collective-permute-start | bytes 393224 | tf_op jit(solution)/shard_map/ppermute | solution.py:238
  83.7 9.0 %collective-permute-start.13 = (f32[256,128]{1,0:T(8,128)S(1)}, f32[256,128]{1,0:T(8,128)S(1)}, u32[]{:S(2)}, u32[]{:S(2)}) collective-permute-start(f32[256,128]{1,0:T(8,128)S(1)} %get-tuple-element.40), channel_id=1, source_target_pairs={{0,4},{1,5},{2,6},{3,7},{4,0},{5,1},{6,2},{7,3},{8,12},{9,13},{10,... | collective-permute-start | bytes 393224 | tf_op jit(solution)/shard_map/ppermute | solution.py:238
